TPU v7x, 512 devices: a whole 4x4x16 slice. The times are simulated.
512 devices in a mesh: tm: 4 (over y), prefix: 128 (over x, z, core).
Axes of the slice: x: 4, y: 4, z: 16, core: 2. Of those that a mesh axis runs over, the one named last changes fastest.
Arguments:
- traffic: bfloat16 [262144, 4096], P('prefix', 'tm'), as said below
- start_level: float32 [262144], P('prefix'), as said below
- subspace: bfloat16 [262144, 64], P('prefix'), as said below
Outputs:
- scores: float32 [64, 4096], P(None, 'tm')
- energy: float32 [4096], P('tm')
Inputs may be any that keep to these rules, and one draw needn't show every extreme that they name: `traffic`: traffic volumes of one prefix pair per bin; each series keeps one typical level across all bins. `start_level`: each series' starting level lies within a factor of two of its typical traffic. `subspace`: each column has about unit length.
All inputs are finite; a program needn't handle non-finite values.
Results may differ from a plain program's by a relative error of at most 0.003.
Values sent between devices are 32-bit elements; how exact they have to be, the bound alone decides.
No kernel may reach another device: no remote copies, remote signals or barrier semaphores. Data moves between devices by JAX's collectives and lax.ppermute only.
A program may use at most 64 MiB of HBM per device.

v0:
```python
import math

import jax
import jax.numpy as jnp
from jax import lax
from jax.sharding import PartitionSpec as P

BLOCK = 256


ewma_rate = 0.002


def entering(x, axis, combine, identity):
    count, place = (lax.axis_size(axis), lax.axis_index(axis))
    everything = jax.tree.map(lambda part: lax.all_gather(part, axis), x)
    start = jax.tree.map(
        lambda part, zero: jnp.broadcast_to(jnp.asarray(zero, part.dtype), part.shape), x, identity
    )

    def lap(k, before):
        reached = k < place
        new = combine(before, jax.tree.map(lambda part: part[k], everything))
        return jax.tree.map(lambda a, b: jnp.where(reached, a, b), new, before)

    return lax.fori_loop(0, count, lap, start)


def combine(earlier, later):
    return (earlier[0] * later[0], later[0] * earlier[1] + later[1])


def shards(traffic, start_level, subspace):
    series, width = traffic.shape
    count_blocks = width // BLOCK
    keep_rate = 1.0 - ewma_rate
    log_keep = math.log(keep_rate)
    offsets = jnp.arange(BLOCK)
    lag_matrix = (offsets[None, :] - offsets[:, None] - 1).astype(jnp.float32)
    strict_qp = jnp.where(
        lag_matrix >= 0.0,
        (ewma_rate * keep_rate ** jnp.maximum(lag_matrix, 0.0)).astype(jnp.bfloat16),
        jnp.zeros((), jnp.bfloat16),
    )
    tail_lags = (BLOCK - 1 - offsets).astype(jnp.float32)
    tail_weights = (ewma_rate * keep_rate**tail_lags).astype(jnp.bfloat16)
    flat_blocks = traffic.reshape(series * count_blocks, BLOCK)
    inner_sum = jnp.dot(flat_blocks, strict_qp, preferred_element_type=jnp.float32)
    block_ends = jnp.dot(flat_blocks, tail_weights, preferred_element_type=jnp.float32).reshape(
        series, count_blocks
    )
    block_ids = jnp.arange(count_blocks).astype(jnp.float32)
    block_gap = block_ids[:, None] - block_ids[None, :] - 1.0
    carry_mix = jnp.where(
        block_gap >= 0, jnp.exp(BLOCK * jnp.maximum(block_gap, 0.0) * log_keep), 0.0
    )
    local_entry = jnp.dot(block_ends, carry_mix.T, precision=lax.Precision.HIGHEST)
    closing_weights = jnp.exp(BLOCK * (count_blocks - 1.0 - block_ids) * log_keep)
    local_close = jnp.dot(block_ends, closing_weights, precision=lax.Precision.HIGHEST)
    factor = jnp.full((1,), math.exp(width * log_keep), jnp.float32)
    identity = (jnp.ones((1,), jnp.float32), jnp.zeros((series,), jnp.float32))
    prefix_factor, prefix_value = entering((factor, local_close), "tm", combine, identity)
    carry_entry = prefix_factor * start_level + prefix_value
    level_entry = (
        local_entry + jnp.exp(BLOCK * block_ids * log_keep)[None, :] * carry_entry[:, None]
    )
    step_powers = jnp.exp(offsets.astype(jnp.float32) * log_keep)
    previous = inner_sum + step_powers[None, :] * level_entry.reshape(series * count_blocks, 1)
    residual = (
        (flat_blocks.astype(jnp.float32) - previous).astype(jnp.bfloat16).reshape(series, width)
    )
    local_scores = lax.dot_general(
        subspace, residual, (((0,), (0,)), ((), ())), preferred_element_type=jnp.float32
    )
    series_total = series * lax.axis_size("prefix")
    scores = lax.psum(local_scores, "prefix")
    scores_low = scores.astype(jnp.bfloat16)
    normal_part = jnp.dot(subspace, scores_low, preferred_element_type=jnp.float32)
    remainder = residual.astype(jnp.float32) - normal_part
    energy = lax.psum(jnp.sum(remainder * remainder, axis=0), "prefix") / series_total
    return (scores, energy)


def solution(mesh):
    return jax.shard_map(
        shards,
        mesh=mesh,
        in_specs=(P("prefix", "tm"), P("prefix"), P("prefix", None)),
        out_specs=(P(None, "tm"), P("tm")),
        check_vma=False,
    )
```

profile of v0, /device:TPU:1, one launch (start us, length us, event | category | flops | bytes accessed | tf_op | source)
XLA Modules:
  0.0 704.0 jit_solution(9338106033665262471)
XLA Ops:
  7.2 0.0 copy-start
  7.2 0.0 all-reduce.3.cloned.1.call-start
  7.3 7.8 %dot_general.28 = bf16[2048,4,256]{2,1,0:T(4,128)(2,1)} reshape(bf16[2048,1024]{1,0:T(8,128)(2,1)} %param.5) | data formatting | bytes 8388608 | tf_op jit(solution)/shard_map/dot_general | solution.py:49
  15.1 7.5 %reshape.38 = bf16[8192,256]{1,0:T(8,128)(2,1)} reshape(bf16[2048,1024]{1,0:T(8,128)(2,1)} %param.5) | data formatting | bytes 8388608 | tf_op jit(solution)/shard_map/reshape | solution.py:47
  22.7 0.0 copy-start.2
  22.7 22.6 %multiply_reduce_fusion = f32[2048,4]{1,0:T(8,128)S(1)} fusion(f32[256]{0:T(256)S(1)} %fusion.24, bf16[2048,4,256]{2,1,0:T(4,128)(2,1)} %dot_general.28), kind=kLoop, calls=%fused_computation.10 | loop fusion | flops 6283264 | bytes 4228096 | tf_op jit(solution)/shard_map/dot_general | solution.py:49
  45.3 1.0 fusion.25
  46.3 10.4 %all-gather = f32[8192]{0:T(1024)S(1)} all-gather(f32[2048]{0:T(1024)S(1)} %bitcast.44), channel_id=2, replica_groups=mesh['tm'=4,'prefix'=128] {'tm'}, dimensions={0}, use_global_device_ids=true | all-gather | bytes 40960 | tf_op jit(solution)/shard_map/all_gather | solution.py:16
  56.7 1.3 dynamic-slice
  57.9 0.8 dynamic-update-slice
  58.7 8.4 %all-reduce = f32[4]{0:T(128)S(1)} all-reduce(f32[4]{0:T(128)S(1)} %dynamic-update-slice), channel_id=1, replica_groups=mesh['tm'=4,'prefix'=128] {'tm'}, use_global_device_ids=true, to_apply=%add | all-reduce | flops 4 | bytes 32
  67.1 8.4 %while.16 = (s32[]{:T(128)}, f32[1]{0:T(128)}, f32[2048]{0:T(1024)S(1)}, s32[]{:T(128)}, f32[4,1]{0,1:T(1,128)S(1)}, /*index=5*/f32[4,2048]{1,0:T(4,128)S(1)}, s32[]{:T(128)}, s32[]{:T(128)}) while((s32[]{:T(128)}, f32[1]{0:T(128)}, f32[2048]{0:T(1024)S(1)}, s32[]{:T(128)}, f32[4,1]{0,1:T(1,128)S(1)}, ...), condition=%wide.region_1.2_spmd.clone, body=%wide.region_0.1_spmd.clone.sunk | while | flops 8198 | bytes 41110 | solution.py:26
  67.1 0.7 constant_dynamic-slice_fusion.4
  67.8 0.7 add_select_fusion.2
  69.2 0.7 constant_dynamic-slice_fusion.4
  69.9 0.7 add_select_fusion.2
  71.3 0.7 constant_dynamic-slice_fusion.4
  72.0 0.7 add_select_fusion.2
  73.4 0.7 constant_dynamic-slice_fusion.4
  74.0 0.7 add_select_fusion.2
  75.5 0.0 copy-done.2
  75.5 1.0 convolution_add_fusion
  76.5 0.4 copy.10
  76.9 0.6 mul.132
  77.5 6.3 copy.9
  83.9 8.0 %fusion.2 = bf16[8192,256]{0,1:T(8,128)(2,1)} fusion(bf16[8192,256]{1,0:T(8,128)(2,1)} %reshape.38, bf16[8192,256]{0,1:T(8,128)(2,1)} %copy.9, f32[8192]{0:T(1024)S(1)} %mul.132, f32[256]{0:T(256)S(1)} %multiply_exponential_fusion), kind=kOutput, calls=%fused_computation.6 | convolution fusion | flops 1084751872 | bytes 12616704 | tf_op jit(solution)/shard_map/dot_general | solution.py:48
  91.9 6.4 copy.11
  98.3 7.5 %reshape.39 = bf16[2048,1024]{1,0:T(8,128)(2,1)} reshape(bf16[8192,256]{1,0:T(8,128)(2,1)} %copy.11) | data formatting | bytes 8388608 | tf_op jit(solution)/shard_map/reshape | solution.py:70
  105.8 0.0 copy-done
  105.8 3.7 convolution_bitcast_fusion.1
  109.5 0.0 all-reduce.3.cloned.1.call-update
  109.6 6.5 copy.12
  116.1 328.3 %all-reduce.3.cloned.1.call-done = f32[64,1024]{1,0:T(8,128)} async-done(((f32[64,1024]{1,0:T(8,128)}), f32[64,1024]{1,0:T(8,128)}) %all-reduce.3.cloned.1.call-update) | async-done | bytes 262160 | tf_op jit(solution)/shard_map/psum | solution.py:76
  444.4 0.0 copy-start.1
  444.4 3.7 fusion.4
  448.2 247.7 %psum.15 = f32[1024]{0:T(1024)S(1)} all-reduce(f32[1024]{0:T(1024)S(1)} %fusion.4), channel_id=1, replica_groups=mesh['tm'=4,'prefix'=128] {'prefix'}, use_global_device_ids=true, to_apply=%region_4.5 | all-reduce | flops 1024 | bytes 8192 | tf_op jit(solution)/shard_map/psum | solution.py:80
  695.9 0.6 broadcast_multiply_fusion
  696.5 0.0 copy-done.1
  696.5 0.7 copy.30
  (12 shorter events, 0.1 us)
Async XLA Ops:
  7.2 98.6 %copy-start = (bf16[2048,64]{0,1:T(8,128)(2,1)S(1)}, bf16[2048,64]{0,1:T(8,128)(2,1)}, u32[]{:S(2)}) copy-start(bf16[2048,64]{0,1:T(8,128)(2,1)} %param.7) | copy-start | bytes 786436
  7.2 437.3 %all-reduce.3.cloned.1.call-start = ((), (), s32[]{:S(2)}) async-start(), calls=%async_computation | async-start | bytes 524288 | tf_op jit(solution)/shard_map/psum | solution.py:76
  22.7 52.8 %copy-start.2 = (f32[2048]{0:T(1024)S(1)}, f32[2048]{0:T(1024)}, u32[]{:S(2)}) copy-start(f32[2048]{0:T(1024)} %param.6) | copy-start | bytes 24580
  444.4 252.0 %copy-start.1 = (f32[64,1024]{1,0:T(8,128)S(1)}, f32[64,1024]{1,0:T(8,128)}, u32[]{:S(2)}) copy-start(f32[64,1024]{1,0:T(8,128)} %all-reduce.3.cloned.1.call-done) | copy-start | bytes 786436
Sparse Core Ops, SparseCore 0:
  109.7 334.7 all-reduce.2
where the time goes:
time: 705 us; the launch traced here: 704 us
  waiting for transfers between devices  328 us (47%)
  blocking collectives  266 us (38%)
  local copies, waits for them, and re-layouts  48.7 us (7%)
  other arithmetic  26 us (4%)
  matrix products  17.5 us (2%)
  between operations  14.1 us (2%)
    psum x1, waiting for transfers between devices, shards(): scores = lax.psum(local_scores, 'prefix')  328 us
    psum x1, blocking collectives, shards(): lax.psum(jnp.sum(remainder * remainder, axis=0), 'prefix') / series_total  248 us
    dot_general x1, other arithmetic, shards(): jnp.dot(flat_blocks, tail_weights, preferred_element_type=jnp.float32)  22.6 us
  transfers between devices with their start and end apart: 1, of which 1 were waited for; matrix products, arithmetic and copies ran while one was open for 1% of the time, Pallas kernels for 0%

commit v1 on v0

v1 whole, which is shorter than its diff:
```python
import functools
import math

import jax
import jax.numpy as jnp
import ml_dtypes
import numpy as np
from jax import lax
from jax.experimental import pallas as pl
from jax.experimental.pallas import tpu as pltpu
from jax.sharding import Mesh, PartitionSpec as P

BLOCK = 256
LANES = 128
K = 64
ewma_rate = 0.002

ROWS = 256
PIECE = 72


def powers(exponents):
    return (1.0 - ewma_rate) ** np.asarray(exponents, np.float64)


def taps():
    return (ewma_rate * powers(np.arange(BLOCK))).astype(ml_dtypes.bfloat16)


def closing_kernel(x_ref, u_ref, w_ref, scale_ref, close_ref, gram_ref):
    ends = jnp.dot(x_ref[...], w_ref[...], preferred_element_type=jnp.float32)
    ends = jnp.transpose(ends * scale_ref[...])
    close = jnp.sum(ends[0:8], axis=0, keepdims=True)
    close_ref[...] = jnp.broadcast_to(close[None], close_ref.shape)

    @pl.when(pl.program_id(0) == 0)
    def _():
        gram_ref[...] = jnp.zeros_like(gram_ref)

    u = u_ref[...]
    gram_ref[...] += lax.dot_general(
        u, u, (((0,), (0,)), ((), ())), preferred_element_type=jnp.float32
    )


def main_kernel(
    shards, width,
    x_ref, u_ref, closes_ref, start_ref, gram_ref, toeplitz_ref, tail_ref, step_ref,
    out_ref, scores_ref, square_ref,
):
    place = lax.axis_index("tm")
    blocks = width // BLOCK

    @pl.when(pl.program_id(0) == 0)
    def _():
        scores_ref[...] = jnp.zeros_like(scores_ref)
        square_ref[...] = jnp.zeros_like(square_ref)

    def weight(table):
        value = jnp.float32(table[0])
        for p in range(1, shards):
            value = jnp.where(place == p, jnp.float32(table[p]), value)
        return value

    level = start_ref[...] * weight([powers(width * p) for p in range(shards)])
    for s in range(shards - 1):
        level += closes_ref[s] * weight(
            [powers(width * (p - 1 - s)) if s < p else 0.0 for p in range(shards)]
        )
    level = jnp.transpose(jnp.broadcast_to(level, (LANES, ROWS)))
    block_keep = jnp.float32(powers(BLOCK))
    u = u_ref[...]
    for b in range(blocks):
        cols = slice(b * BLOCK, (b + 1) * BLOCK)
        x = x_ref[:, cols]
        inner = jnp.dot(x, toeplitz_ref[...], preferred_element_type=jnp.float32)
        previous = inner + jnp.concatenate([level, level], axis=1) * step_ref[...]
        residual = (x.astype(jnp.float32) - previous).astype(jnp.bfloat16)
        exact = residual.astype(jnp.float32)
        square_ref[:, cols] += jnp.sum((exact * exact).reshape(ROWS // 8, 8, BLOCK), axis=0)
        scores_ref[:, cols] += lax.dot_general(
            u, residual, (((0,), (0,)), ((), ())), preferred_element_type=jnp.float32
        )
        if b + 1 < blocks:
            level = (
                jnp.dot(x, tail_ref[...], preferred_element_type=jnp.float32) + block_keep * level
            )

    @pl.when(pl.program_id(0) == pl.num_programs(0) - 1)
    def _():
        pieces = width // LANES
        per = K // pieces
        square = jnp.sum(square_ref[...], axis=0, keepdims=True)
        gram = gram_ref[...]
        empty = jnp.zeros((per // 2, LANES - K), jnp.float32)
        for j in range(pieces):
            cols = slice(j * LANES, (j + 1) * LANES)
            out_ref[j, 0:K] = scores_ref[:, cols]
            out_ref[j, K : K + 1] = square[:, cols]
            first, second = gram[j * per : j * per + per // 2], gram[j * per + per // 2 : (j + 1) * per]
            out_ref[j, K + 1 : K + 1 + per // 2] = jnp.concatenate([first, second], axis=1)
            out_ref[j, K + 1 + per // 2 :] = jnp.zeros((PIECE - K - 1 - per // 2, LANES), jnp.float32)


def energy_kernel(series, in_ref, scores_ref, energy_ref):
    pieces = in_ref.shape[0]
    half = K // pieces // 2
    rows = []
    for j in range(pieces):
        packed = in_ref[j, K + 1 : K + 1 + half]
        rows += [packed[:, :K], packed[:, K:]]
    gram = jnp.concatenate(rows, axis=0)
    high = gram.astype(jnp.bfloat16)
    rest = gram - high.astype(jnp.float32)
    middle = rest.astype(jnp.bfloat16)
    low = (rest - middle.astype(jnp.float32)).astype(jnp.bfloat16)
    for j in range(pieces):
        cols = slice(j * LANES, (j + 1) * LANES)
        scores = in_ref[j, 0:K]
        scores_ref[:, cols] = scores
        scores_low = scores.astype(jnp.bfloat16)
        spread = jnp.dot(high, scores_low, preferred_element_type=jnp.float32)
        spread += jnp.dot(middle, scores_low, preferred_element_type=jnp.float32)
        spread += jnp.dot(low, scores_low, preferred_element_type=jnp.float32)
        inside = jnp.sum(
            scores_low.astype(jnp.float32) * (2.0 * scores - spread), axis=0, keepdims=True
        )
        energy_ref[:, cols] = (in_ref[j, K : K + 1] - inside) * jnp.float32(1.0 / series)


def shards_fn(shards, total, traffic, start_level, subspace):
    series, width = traffic.shape
    blocks = width // BLOCK
    pieces = width // LANES
    tap = taps()
    closing = np.zeros((width, LANES), ml_dtypes.bfloat16)
    for b in range(blocks):
        closing[b * BLOCK : (b + 1) * BLOCK, b] = tap[::-1]
    scale = np.zeros((1, LANES), np.float32)
    scale[0, :blocks] = powers(BLOCK * (blocks - 1 - np.arange(blocks)))
    lag = np.arange(BLOCK)[None, :] - np.arange(BLOCK)[:, None] - 1
    toeplitz = np.where(lag >= 0, tap[np.maximum(lag, 0)], tap[0] * 0)
    tail = np.broadcast_to(tap[::-1, None], (BLOCK, LANES))
    step = powers(np.arange(BLOCK))[None, :].astype(np.float32)
    steps = series // ROWS

    def whole(shape):
        return pl.BlockSpec(shape, lambda i: (0,) * len(shape))

    x_spec = pl.BlockSpec((ROWS, width), lambda i: (i, 0))
    u_spec = pl.BlockSpec((ROWS, K), lambda i: (i, 0))
    line_spec = pl.BlockSpec((shards, 1, ROWS), lambda i: (0, 0, i))
    close, gram = pl.pallas_call(
        closing_kernel,
        grid=(steps,),
        in_specs=[x_spec, u_spec, whole((width, LANES)), whole((1, LANES))],
        out_specs=[line_spec, whole((K, K))],
        out_shape=[
            jax.ShapeDtypeStruct((shards, 1, series), jnp.float32),
            jax.ShapeDtypeStruct((K, K), jnp.float32),
        ],
        name="closing",
    )(traffic, subspace, jnp.asarray(closing), jnp.asarray(scale))
    closes = lax.all_to_all(close, "tm", 0, 0, tiled=True)
    part = pl.pallas_call(
        functools.partial(main_kernel, shards, width),
        grid=(steps,),
        in_specs=[
            x_spec, u_spec, line_spec, pl.BlockSpec((1, ROWS), lambda i: (0, i)), whole((K, K)),
            whole((BLOCK, BLOCK)), whole((BLOCK, LANES)), whole((1, BLOCK)),
        ],
        out_specs=whole((pieces, PIECE, LANES)),
        out_shape=jax.ShapeDtypeStruct((pieces, PIECE, LANES), jnp.float32),
        scratch_shapes=[pltpu.VMEM((K, width), jnp.float32), pltpu.VMEM((8, width), jnp.float32)],
        compiler_params=pltpu.CompilerParams(vmem_limit_bytes=32 * 1024 * 1024),
        name="residuals",
    )(
        traffic, subspace, closes, start_level.reshape(1, series), gram,
        jnp.asarray(toeplitz), jnp.asarray(tail), jnp.asarray(step),
    )
    mine = jnp.sum(lax.all_to_all(part, ("x", "core"), 0, 0, tiled=True), axis=0)
    mine = jnp.sum(lax.all_gather(mine, "z"), axis=0)
    every = lax.all_to_all(
        jnp.broadcast_to(mine[None], (pieces, PIECE, LANES)), ("x", "core"), 0, 0, tiled=True
    )
    scores, energy = pl.pallas_call(
        functools.partial(energy_kernel, total),
        out_shape=[
            jax.ShapeDtypeStruct((K, width), jnp.float32),
            jax.ShapeDtypeStruct((1, width), jnp.float32),
        ],
        name="energies",
    )(every)
    return scores, energy.reshape(width)


def solution(mesh):
    times = mesh.shape["tm"]
    fine = Mesh(mesh.devices.reshape(times, 4, 16, 2), ("tm", "x", "z", "core"))
    prefix = ("x", "z", "core")

    def program(traffic, start_level, subspace):
        return jax.shard_map(
            functools.partial(shards_fn, times, traffic.shape[0]),
            mesh=fine,
            in_specs=(P(prefix, "tm"), P(prefix), P(prefix, None)),
            out_specs=(P(None, "tm"), P("tm")),
            check_vma=False,
        )(traffic, start_level, subspace)

    return program
```

time: 705 us -> 97.2 us (0.14)
  waiting for transfers between devices: 328 us -> 0 us
  blocking collectives: 266 us -> 72.8 us
  local copies, waits for them, and re-layouts: 48.7 us -> 5.1 us
  other arithmetic: 26 us -> 0.06 us
  Pallas kernels: 0 us -> 17.9 us
  matrix products: 17.5 us -> 0 us
  between operations: 14.1 us -> 0.73 us
    psum x1 -> x0, waiting for transfers between devices: 328 us -> none  [shards(): scores = lax.psum(local_scores, 'prefix')]
    psum x1 -> x0, blocking collectives: 248 us -> none  [shards(): lax.psum(jnp.sum(remainder * remainder, axis=0), 'prefix') / series_total]
    all_to_all x0 -> x3, blocking collectives: none -> 43.1 us  [the longest x1 17.9 us: shards_fn(): lax.all_to_all(jnp.broadcast_to(mine[None], (pieces, PIECE, LANES)), ('x'...]
    reshape x4 -> x0, local copies, waits for them, and re-layouts: 28 us -> none  [the longest x2 14.1 us: shards(): (flat_blocks.astype(jnp.float32) - previous).astype(jnp.bfloat16)]
    dot_general x1 -> x0, other arithmetic: 22.6 us -> none  [shards(): jnp.dot(flat_blocks, tail_weights, preferred_element_type=jnp.float32)]
    all_gather x1, blocking collectives: 10.4 us -> 29.7 us  [shards_fn(): mine = jnp.sum(lax.all_gather(mine, 'z'), axis=0)]
    pallas_call x0 -> x3, Pallas kernels: none -> 17.9 us  [the longest x1 8.33 us: shards_fn(): pl.pallas_call(functools.partial(main_kernel, shards, width), grid=(steps...]
    dot_general x5 -> x0, matrix products: 17.5 us -> none  [the longest x1 8.02 us: shards(): jnp.dot(flat_blocks, strict_qp, preferred_element_type=jnp.float32)]
  transfers between devices with their start and end apart: 1 -> 0, of which waited for: 1 -> 0; matrix products, arithmetic and copies ran while one was open for 1% -> 0% of each run, Pallas kernels for 0% -> 0%
where the time goes in v1:
time: 97.2 us; the launch traced here: 96.6 us
  blocking collectives  72.8 us (75%)
  Pallas kernels  17.9 us (18%)
  local copies, waits for them, and re-layouts  5.1 us (5%)
    all_gather x1, blocking collectives, shards_fn(): mine = jnp.sum(lax.all_gather(mine, 'z'), axis=0)  29.7 us
    all_to_all x1, blocking collectives, shards_fn(): lax.all_to_all(jnp.broadcast_to(mine[None], (pieces, PIECE, LANES)), ('x'...  17.9 us
    all_to_all x1, blocking collectives, shards_fn(): lax.all_to_all(part, ('x', 'core'), 0, 0, tiled=True)  15.9 us
    all_to_all x1, blocking collectives, shards_fn(): closes = lax.all_to_all(close, 'tm', 0, 0, tiled=True)  9.31 us
    pallas_call x1, Pallas kernels, shards_fn(): pl.pallas_call(functools.partial(main_kernel, shards, width), grid=(steps...  8.33 us
    pallas_call x1, Pallas kernels, shards_fn(): pl.pallas_call(closing_kernel, grid=(steps,), in_specs=[x_spec, u_spec, w...  7.67 us
    unnamed x15, local copies, waits for them, and re-layouts  4.98 us

profile of v1, /device:TPU:1, one launch (start us, length us, event | category | flops | bytes accessed | tf_op | source)
XLA Modules:
  0.0 96.6 jit_solution(10644248421012528763)
XLA Ops:
  0.6 0.0 copy-start.5
  0.6 0.0 copy-start.2
  0.7 0.0 copy-start.6
  0.7 0.0 copy-start.4
  0.7 2.0 %copy.13.u_ref = bf16[2048,64]{1,0:T(8,128)(2,1)} copy(bf16[2048,64]{0,1:T(8,128)(2,1)} %param.10) | data formatting | bytes 524288 | tf_op args[2]
  2.7 0.0 copy-start.1
  2.7 7.7 %closing.1 = (f32[4,1,2048]{2,1,0:T(1,128)}, f32[64,64]{1,0:T(8,128)}) custom-call(bf16[2048,1024]{1,0:T(8,128)(2,1)} %x_ref.3, bf16[2048,64]{1,0:T(8,128)(2,1)} %copy.13.u_ref, bf16[1024,128]{1,0:T(8,128)(2,1)} %constant.12.clone.w_ref, f32[1,128]{1,0:T(1,128)} %constant.13.clone.scale_ref), custom_call_target="tpu_custom_call" | custom-call | tf_op jit(solution)/shard_map/closing/pallas_call | solution.py:153
  10.4 9.3 %all_to_all.15.closes_ref = f32[4,1,2048]{2,1,0:T(1,128)S(1)} all-to-all(f32[4,1,2048]{2,1,0:T(1,128)} %get-tuple-element.6), channel_id=1, replica_groups=mesh['tm'=4,'x'=4,'z'=16,'core'=2] {'tm'}, dimensions={0} | all-to-all | bytes 65536 | tf_op jit(solution)/shard_map/all_to_all | solution.py:164
  19.7 0.0 copy-done.6
  19.7 0.1 jit_solution_.3.tail_ref
  19.8 0.0 copy-done.5
  19.8 0.0 copy-done.2
  19.8 0.0 copy-done.4
  19.8 0.0 copy-done.1
  19.8 0.0 copy-start
  19.8 2.2 %copy-done = bf16[2048,1024]{1,0:T(8,128)(2,1)S(1)} copy-done((bf16[2048,1024]{1,0:T(8,128)(2,1)S(1)}, bf16[2048,1024]{1,0:T(8,128)(2,1)}, u32[]{:S(2)}) %copy-start) | copy-done | bytes 4194328
  22.0 0.0 copy-start.3
  22.0 0.8 copy-done.3
  22.8 8.3 %residuals.1 = f32[8,72,128]{2,1,0:T(8,128)S(1)} custom-call(bf16[2048,1024]{1,0:T(8,128)(2,1)S(1)} %copy-done, bf16[2048,64]{1,0:T(8,128)(2,1)S(1)} %copy-done.1, f32[4,1,2048]{2,1,0:T(1,128)S(1)} %all_to_all.15.closes_ref, f32[1,2048]{1,0:T(1,128)S(1)} %bitcast.3, f32[64,64]{1,0:T(8,128)S(1)} %copy-done.3, bf16[256,256]{1,0:T(8,128)(2,1)S(1)} %copy-done.2, ...), custom_call_target="tpu_custom_call" | custom-call | tf_op jit(solution)/shard_map/residuals/pallas_call | solution.py:165
  31.1 15.9 %all_to_all.16 = f32[8,72,128]{2,1,0:T(8,128)S(1)} all-to-all(f32[8,72,128]{2,1,0:T(8,128)S(1)} %residuals.1), channel_id=1, replica_groups=mesh['tm'=4,'x'=4,'z'=16,'core'=2] {'x','core'}, dimensions={0} | all-to-all | bytes 589824 | tf_op jit(solution)/shard_map/all_to_all | solution.py:181
  47.1 29.7 %all-gather = f32[1152,128]{1,0:T(8,128)S(1)} all-gather(f32[72,128]{1,0:T(8,128)S(1)} %reduce_sum.18), channel_id=2, replica_groups=mesh['tm'=4,'x'=4,'z'=16,'core'=2] {'z'}, dimensions={0}, use_global_device_ids=true | all-gather | bytes 626688 | tf_op jit(solution)/shard_map/all_gather | solution.py:182
  76.8 17.9 %all_to_all.17.in_ref = f32[8,72,128]{2,1,0:T(8,128)} all-to-all(f32[8,72,128]{2,1,0:T(8,128)S(1)} %broadcast_in_dim.2), channel_id=1, replica_groups=mesh['tm'=4,'x'=4,'z'=16,'core'=2] {'x','core'}, dimensions={0} | all-to-all | bytes 589824 | tf_op jit(solution)/shard_map/all_to_all | solution.py:183
  94.7 1.9 %energies.1 = (f32[64,1024]{1,0:T(8,128)}, f32[1,1024]{1,0:T(1,128)}) custom-call(f32[8,72,128]{2,1,0:T(8,128)} %all_to_all.17.in_ref), custom_call_target="tpu_custom_call" | custom-call | tf_op jit(solution)/shard_map/energies/pallas_call | solution.py:186
  (3 shorter events, 0.1 us)
Async XLA Ops:
  0.6 19.2 %copy-start.5 = (f32[1,256]{1,0:T(1,128)S(1)}, f32[1,256]{1,0:T(1,128)}, u32[]{:S(2)}) copy-start(f32[1,256]{1,0:T(1,128)} %constant.16.clone.step_ref) | copy-start | bytes 3076
  0.6 19.2 %copy-start.2 = (bf16[256,256]{1,0:T(8,128)(2,1)S(1)}, bf16[256,256]{1,0:T(8,128)(2,1)}, u32[]{:S(2)}) copy-start(bf16[256,256]{1,0:T(8,128)(2,1)} %constant.14.clone.toeplitz_ref) | copy-start | bytes 393220
  0.7 19.0 %copy-start.6 = (bf16[256]{0:T(256)(128)(2,1)S(1)}, bf16[256]{0:T(256)(128)(2,1)}, u32[]{:S(2)}) copy-start(bf16[256]{0:T(256)(128)(2,1)} %constant.15.clone) | copy-start | bytes 1540
  0.7 19.1 %copy-start.4 = (f32[2048]{0:T(1024)S(1)}, f32[2048]{0:T(1024)}, u32[]{:S(2)}) copy-start(f32[2048]{0:T(1024)} %param.9) | copy-start | bytes 24580
  2.7 17.1 %copy-start.1 = (bf16[2048,64]{1,0:T(8,128)(2,1)S(1)}, bf16[2048,64]{1,0:T(8,128)(2,1)}, u32[]{:S(2)}) copy-start(bf16[2048,64]{1,0:T(8,128)(2,1)} %copy.13.u_ref) | copy-start | bytes 786436
  19.8 2.2 %copy-start = (bf16[2048,1024]{1,0:T(8,128)(2,1)S(1)}, bf16[2048,1024]{1,0:T(8,128)(2,1)}, u32[]{:S(2)}) copy-start(bf16[2048,1024]{1,0:T(8,128)(2,1)} %x_ref.3) | copy-start | bytes 12582916
  22.0 0.8 copy-start.3

commit v2 on v0

v2 whole, which is shorter than its diff:
```python
import functools

import jax
import jax.numpy as jnp
import ml_dtypes
import numpy as np
from jax import lax
from jax.experimental import pallas as pl
from jax.experimental.pallas import tpu as pltpu
from jax.sharding import Mesh, PartitionSpec as P

BLOCK=256; LANES=128; K=64; ewma_rate=0.002
PIECE=40
def powers(e): return (1.0-ewma_rate)**np.asarray(e,np.float64)
def taps(): return (ewma_rate*powers(np.arange(BLOCK))).astype(ml_dtypes.bfloat16)

def closing_kernel(rows, x_hbm, tail_ref, close_ref, x_ref, sems):
    series, width = x_ref.shape
    blocks = width // BLOCK
    steps = series // rows
    copies=[pltpu.make_async_copy(x_hbm.at[pl.ds(i*rows,rows)], x_ref.at[pl.ds(i*rows,rows)], sems.at[i]) for i in range(steps)]
    for c in copies: c.start()
    tail=tail_ref[...]
    for i in range(steps):
        copies[i].wait()
        total=None
        for b in range(blocks):
            end=jnp.dot(x_ref[i*rows:(i+1)*rows, b*BLOCK:(b+1)*BLOCK], tail, preferred_element_type=jnp.float32)
            end=end*jnp.float32(powers(BLOCK*(blocks-1-b))) if b+1<blocks else end
            total=end if total is None else total+end
        line=jnp.transpose(total)[0:1]
        close_ref[:,:,i*rows:(i+1)*rows]=jnp.broadcast_to(line[None],(close_ref.shape[0],1,rows))

def main_kernel(shards, rows, unroll, x_ref, ut_ref, closes_ref, start_ref, toeplitz_ref, tail_ref, step_ref, out_ref, scores_ref, square_ref):
    series, width = x_ref.shape
    blocks = width // BLOCK
    place = lax.axis_index("tm")
    def weight(table):
        value=jnp.float32(table[0])
        for p in range(1,shards):
            value=jnp.where(place==p, jnp.float32(table[p]), value)
        return value
    w0=weight([powers(width*p) for p in range(shards)])
    ws=[weight([powers(width*(p-1-s)) if s<p else 0.0 for p in range(shards)]) for s in range(shards-1)]
    basis=ut_ref[...]
    gram=lax.dot_general(basis,basis,(((1,),(1,)),((),())),preferred_element_type=jnp.float32)
    scores_ref[...]=jnp.zeros_like(scores_ref)
    square_ref[...]=jnp.zeros_like(square_ref)
    block_keep=jnp.float32(powers(BLOCK))
    toeplitz=toeplitz_ref[...]; tail=tail_ref[...]; step=step_ref[...]
    def lap(i, carry):
        at=pl.ds(pl.multiple_of(i*rows,rows),rows)
        line=start_ref[:,at]*w0
        for s in range(shards-1):
            line+=closes_ref[s,:,at]*ws[s]
        level=jnp.transpose(jnp.broadcast_to(line,(LANES,rows)))
        ut=ut_ref[:,at]
        for b in range(blocks):
            cols=slice(b*BLOCK,(b+1)*BLOCK)
            x=x_ref[at,cols]
            inner=jnp.dot(x,toeplitz,preferred_element_type=jnp.float32)
            previous=inner+jnp.concatenate([level,level],axis=1)*step
            residual=(x.astype(jnp.float32)-previous).astype(jnp.bfloat16)
            exact=residual.astype(jnp.float32)
            square_ref[:,cols]+=jnp.sum((exact*exact).reshape(rows//8,8,BLOCK),axis=0)
            scores_ref[:,cols]+=jnp.dot(ut,residual,preferred_element_type=jnp.float32)
            if b+1<blocks:
                level=jnp.dot(x,tail,preferred_element_type=jnp.float32)+block_keep*level
        return carry
    lax.fori_loop(0,series//rows,lap,0,unroll=unroll)
    square=jnp.sum(square_ref[...],axis=0,keepdims=True)
    pieces=out_ref.shape[0]
    halves=pieces*LANES//width
    high=K//halves; per=K//pieces
    out_ref[:, high:, :]=jnp.zeros((pieces,PIECE-high,LANES),jnp.float32)
    for p in range(pieces):
        j,h=divmod(p,halves)
        cols=slice(j*LANES,(j+1)*LANES)
        out_ref[p,0:high]=scores_ref[h*high:(h+1)*high,cols]
        out_ref[p,high:high+per,0:K]=gram[p*per:(p+1)*per]
        out_ref[p,high+per:high+per+1]=square[:,cols]

def energy_kernel(series, in_ref, scores_ref, energy_ref):
    pieces=in_ref.shape[0]
    width=scores_ref.shape[1]
    halves=pieces*LANES//width
    high=K//halves; per=K//pieces
    gram=jnp.concatenate([in_ref[p,high:high+per,0:K] for p in range(pieces)],axis=0)
    top=gram.astype(jnp.bfloat16)
    rest=gram-top.astype(jnp.float32)
    middle=rest.astype(jnp.bfloat16)
    low=(rest-middle.astype(jnp.float32)).astype(jnp.bfloat16)
    for j in range(width//LANES):
        for h in range(halves):
            scores_ref[h*high:(h+1)*high,j*LANES:(j+1)*LANES]=in_ref[j*halves+h,0:high]
        energy_ref[:,j*LANES:(j+1)*LANES]=in_ref[j*halves,high+per:high+per+1]
    scores=scores_ref[...]
    scores_low=scores.astype(jnp.bfloat16)
    spread=jnp.dot(jnp.concatenate([top,middle,low],axis=0),scores_low,preferred_element_type=jnp.float32)
    spread=spread[0:K]+spread[K:2*K]+spread[2*K:]
    inside=jnp.sum(scores_low.astype(jnp.float32)*(2.0*scores-spread),axis=0,keepdims=True)
    energy_ref[...]=(energy_ref[...]-inside)*jnp.float32(1.0/series)

def consts():
    tap=taps()
    lag=np.arange(BLOCK)[None,:]-np.arange(BLOCK)[:,None]-1
    toeplitz=np.where(lag>=0,tap[np.maximum(lag,0)],tap[0]*0).astype(ml_dtypes.bfloat16)
    tail=np.broadcast_to(tap[::-1,None],(BLOCK,LANES))
    step=powers(np.arange(BLOCK))[None,:].astype(np.float32)
    return jnp.asarray(toeplitz),jnp.asarray(tail),jnp.asarray(step)

def call_closing(rows,shards,traffic,tail):
    series,width=traffic.shape
    vm=pl.BlockSpec(memory_space=pltpu.VMEM)
    return pl.pallas_call(functools.partial(closing_kernel,rows),
        in_specs=[pl.BlockSpec(memory_space=pltpu.HBM),vm],
        out_specs=[vm]*2,
        out_shape=[jax.ShapeDtypeStruct((shards,1,series),jnp.float32),pltpu.VMEM((series,width),jnp.bfloat16)],
        scratch_shapes=[pltpu.SemaphoreType.DMA((series//rows,))],
        compiler_params=pltpu.CompilerParams(vmem_limit_bytes=48*1024*1024),
        name="closing")(traffic,tail)
def call_main(rows,unroll,shards,pieces,xv,ut,closes,start,toeplitz,tail,step):
    series,width=xv.shape
    vm=pl.BlockSpec(memory_space=pltpu.VMEM)
    return pl.pallas_call(functools.partial(main_kernel,shards,rows,unroll),
        in_specs=[vm]*7,out_specs=vm,out_shape=jax.ShapeDtypeStruct((pieces,PIECE,LANES),jnp.float32),
        scratch_shapes=[pltpu.VMEM((K,width),jnp.float32),pltpu.VMEM((8,width),jnp.float32)],
        compiler_params=pltpu.CompilerParams(vmem_limit_bytes=48*1024*1024),
        name="residuals")(xv,ut,closes,start,toeplitz,tail,step)
def call_energy(total,width,every):
    vm=pl.BlockSpec(memory_space=pltpu.VMEM)
    return pl.pallas_call(functools.partial(energy_kernel,total),
        in_specs=[vm],out_specs=[vm,vm],
        out_shape=[jax.ShapeDtypeStruct((K,width),jnp.float32),jax.ShapeDtypeStruct((1,width),jnp.float32)],
        name="energies")(pltpu.with_memory_space_constraint(every,pltpu.VMEM))

ROWS_CLOSING = 512
ROWS_MAIN = 2048
GROUP = ("x", "near", "core")


def shards_fn(shards, total, traffic, start_level, subspace):
    series, width = traffic.shape
    pieces = 1
    for axis in GROUP:
        pieces *= lax.axis_size(axis)
    toeplitz, tail, step = consts()
    close, kept = call_closing(ROWS_CLOSING, shards, traffic, tail)
    closes = lax.all_to_all(close, "tm", 0, 0, tiled=True)
    part = call_main(
        ROWS_MAIN, 1, shards, pieces,
        kept, subspace.T, closes, start_level.reshape(1, series), toeplitz, tail, step,
    )
    mine = jnp.sum(lax.all_to_all(part, GROUP, 0, 0, tiled=True), axis=0)
    far = lax.axis_size("far")
    mine = jnp.sum(
        lax.all_to_all(jnp.broadcast_to(mine[None], (far,) + mine.shape), "far", 0, 0, tiled=True), axis=0
    )
    every = lax.all_to_all(
        jnp.broadcast_to(mine[None], (pieces,) + mine.shape), GROUP, 0, 0, tiled=True
    )
    scores, energy = call_energy(total, width, every)
    return scores, energy.reshape(width)


def solution(mesh):
    times = mesh.shape["tm"]
    fine = Mesh(mesh.devices.reshape(times, 4, 8, 2, 2), ("tm", "x", "far", "near", "core"))
    prefix = ("x", "far", "near", "core")

    def program(traffic, start_level, subspace):
        return jax.shard_map(
            functools.partial(shards_fn, times, traffic.shape[0]),
            mesh=fine,
            in_specs=(P(prefix, "tm"), P(prefix), P(prefix, None)),
            out_specs=(P(None, "tm"), P("tm")),
            check_vma=False,
        )(traffic, start_level, subspace)

    return program
```

time: 705 us -> 76.6 us (0.11)
  waiting for transfers between devices: 328 us -> 0 us
  blocking collectives: 266 us -> 67.1 us
  local copies, waits for them, and re-layouts: 48.7 us -> 0.86 us
  other arithmetic: 26 us -> 0.04 us
  matrix products: 17.5 us -> 0 us
  between operations: 14.1 us -> 0.72 us
  Pallas kernels: 0 us -> 7.7 us
    psum x1 -> x0, waiting for transfers between devices: 328 us -> none  [shards(): scores = lax.psum(local_scores, 'prefix')]
    psum x1 -> x0, blocking collectives: 248 us -> none  [shards(): lax.psum(jnp.sum(remainder * remainder, axis=0), 'prefix') / series_total]
    all_to_all x0 -> x4, blocking collectives: none -> 67.1 us  [the longest x1 28.1 us: shards_fn(): lax.all_to_all(jnp.broadcast_to(mine[None], (far,) + mine.shape), 'far',...]
    reshape x4 -> x0, local copies, waits for them, and re-layouts: 28 us -> none  [the longest x2 14.1 us: shards(): (flat_blocks.astype(jnp.float32) - previous).astype(jnp.bfloat16)]
    dot_general x1 -> x0, other arithmetic: 22.6 us -> none  [shards(): jnp.dot(flat_blocks, tail_weights, preferred_element_type=jnp.float32)]
    dot_general x5 -> x0, matrix products: 17.5 us -> none  [the longest x1 8.02 us: shards(): jnp.dot(flat_blocks, strict_qp, preferred_element_type=jnp.float32)]
    all_gather x1 -> x0, blocking collectives: 10.4 us -> none  [entering(): everything = jax.tree.map(lambda part: lax.all_gather(part, axis), x)]
    unnamed x1 -> x0, blocking collectives: 8.39 us -> none
  transfers between devices with their start and end apart: 1 -> 0, of which waited for: 1 -> 0; matrix products, arithmetic and copies ran while one was open for 1% -> 0% of each run, Pallas kernels for 0% -> 0%
where the time goes in v2:
time: 76.6 us; the launch traced here: 76.4 us
  blocking collectives  67.1 us (88%)
  Pallas kernels  7.7 us (10%)
  local copies, waits for them, and re-layouts  0.86 us (1%)
    all_to_all x1, blocking collectives, shards_fn(): lax.all_to_all(jnp.broadcast_to(mine[None], (far,) + mine.shape), 'far',...  28.1 us
    all_to_all x1, blocking collectives, shards_fn(): mine = jnp.sum(lax.all_to_all(part, GROUP, 0, 0, tiled=True), axis=0)  15.8 us
    all_to_all x1, blocking collectives, shards_fn(): lax.all_to_all(jnp.broadcast_to(mine[None], (pieces,) + mine.shape), GROU...  14.1 us
    all_to_all x1, blocking collectives, shards_fn(): closes = lax.all_to_all(close, 'tm', 0, 0, tiled=True)  9.11 us
    pallas_call x1, Pallas kernels, call_main(): pl.pallas_call(functools.partial(main_kernel, shards, rows, unroll), in_s...  3.61 us
    pallas_call x1, Pallas kernels, call_closing(): pl.pallas_call(functools.partial(closing_kernel, rows), in_specs=[pl.Bloc...  3.19 us

profile of v2, /device:TPU:1, one launch (start us, length us, event | category | flops | bytes accessed | tf_op | source)
XLA Modules:
  0.0 76.4 jit_solution(16822289353476196191)
XLA Ops:
  0.6 0.0 copy-start.3
  0.6 0.0 copy-start.1
  0.7 0.0 copy-start
  0.7 0.0 copy-start.2
  0.7 0.8 %jit_solution_.3.tail_ref = bf16[256,128]{1,0:T(8,128)(2,1)S(1)} broadcast(bf16[256]{0:T(256)(128)(2,1)} %constant.9.clone), dimensions={0} | broadcast | bytes 66048 | tf_op jit(solution)
  1.5 3.2 %closing.1 = (f32[4,1,2048]{2,1,0:T(1,128)S(1)}, bf16[2048,1024]{1,0:T(8,128)(2,1)S(1)}) custom-call(bf16[2048,1024]{1,0:T(8,128)(2,1)} %x_hbm.1, bf16[256,128]{1,0:T(8,128)(2,1)S(1)} %jit_solution_.3.tail_ref), custom_call_target="tpu_custom_call" | custom-call | tf_op jit(solution)/shard_map/closing/pallas_call | solution.py:115
  4.7 9.1 %all_to_all.20.closes_ref = f32[4,1,2048]{2,1,0:T(1,128)S(1)} all-to-all(f32[4,1,2048]{2,1,0:T(1,128)S(1)} %get-tuple-element.7), channel_id=1, replica_groups=mesh['tm'=4,'x'=4,'far'=8,'near'=2,'core'=2] {'tm'}, dimensions={0} | all-to-all | bytes 65536 | tf_op jit(solution)/shard_map/all_to_all | solution.py:149
  13.8 0.0 copy-done.3
  13.8 0.0 copy-done.1
  13.8 0.0 copy-done
  13.8 0.0 copy-done.2
  13.8 3.6 %residuals.1 = f32[16,40,128]{2,1,0:T(8,128)S(1)} custom-call(bf16[2048,1024]{1,0:T(8,128)(2,1)S(1)} %get-tuple-element.6.x_ref, bf16[64,2048]{1,0:T(8,128)(2,1)S(1)} %bitcast.3, f32[4,1,2048]{2,1,0:T(1,128)S(1)} %all_to_all.20.closes_ref, f32[1,2048]{1,0:T(1,128)S(1)} %bitcast.4, bf16[256,256]{1,0:T(8,128)(2,1)S(1)} %copy-done.1, ...), custom_call_target="tpu_custom_call" | custom-call | tf_op jit(solution)/shard_map/residuals/pallas_call | solution.py:125
  17.4 15.8 %all_to_all.21 = f32[16,40,128]{2,1,0:T(8,128)S(1)} all-to-all(f32[16,40,128]{2,1,0:T(8,128)S(1)} %residuals.1), channel_id=1, replica_groups=mesh['tm'=4,'x'=4,'far'=8,'near'=2,'core'=2] {'x','near','core'}, dimensions={0} | all-to-all | bytes 655360 | tf_op jit(solution)/shard_map/all_to_all | solution.py:154
  33.2 28.1 %all_to_all.22 = f32[8,40,128]{2,1,0:T(8,128)S(1)} all-to-all(f32[8,40,128]{2,1,0:T(8,128)S(1)} %broadcast_in_dim.4), channel_id=1, replica_groups=mesh['tm'=4,'x'=4,'far'=8,'near'=2,'core'=2] {'far'}, dimensions={0} | all-to-all | bytes 327680 | tf_op jit(solution)/shard_map/all_to_all | solution.py:157
  61.4 14.1 %all_to_all.23.in_ref = f32[16,40,128]{2,1,0:T(8,128)S(1)} all-to-all(f32[16,40,128]{2,1,0:T(8,128)S(1)} %broadcast_in_dim.5), channel_id=1, replica_groups=mesh['tm'=4,'x'=4,'far'=8,'near'=2,'core'=2] {'x','near','core'}, dimensions={0} | all-to-all | bytes 655360 | tf_op jit(solution)/shard_map/all_to_all | solution.py:159
  75.5 0.9 %energies.1 = (f32[64,1024]{1,0:T(8,128)}, f32[1,1024]{1,0:T(1,128)}) custom-call(f32[16,40,128]{2,1,0:T(8,128)S(1)} %all_to_all.23.in_ref), custom_call_target="tpu_custom_call" | custom-call | tf_op jit(solution)/shard_map/energies/pallas_call | solution.py:132
  (4 shorter events, 0.1 us)
Async XLA Ops:
  0.6 13.2 %copy-start.3 = (f32[1,256]{1,0:T(1,128)S(1)}, f32[1,256]{1,0:T(1,128)}, u32[]{:S(2)}) copy-start(f32[1,256]{1,0:T(1,128)} %constant.10.clone.step_ref) | copy-start | bytes 3076
  0.6 13.2 %copy-start.1 = (bf16[256,256]{1,0:T(8,128)(2,1)S(1)}, bf16[256,256]{1,0:T(8,128)(2,1)}, u32[]{:S(2)}) copy-start(bf16[256,256]{1,0:T(8,128)(2,1)} %constant.8.clone.toeplitz_ref) | copy-start | bytes 393220
  0.7 13.2 %copy-start = (bf16[2048,64]{0,1:T(8,128)(2,1)S(1)}, bf16[2048,64]{0,1:T(8,128)(2,1)}, u32[]{:S(2)}) copy-start(bf16[2048,64]{0,1:T(8,128)(2,1)} %param.8) | copy-start | bytes 786436
  0.7 13.1 %copy-start.2 = (f32[2048]{0:T(1024)S(1)}, f32[2048]{0:T(1024)}, u32[]{:S(2)}) copy-start(f32[2048]{0:T(1024)} %param.7) | copy-start | bytes 24580

commit v3 on v0

v3 whole, which is shorter than its diff:
```python
import functools

import jax
import jax.numpy as jnp
import ml_dtypes
import numpy as np
from jax import lax
from jax.experimental import pallas as pl
from jax.experimental.pallas import tpu as pltpu
from jax.sharding import Mesh, PartitionSpec as P

BLOCK = 256
LANES = 128
SUBLANES = 4
K = 64
ewma_rate = 0.002


def powers(exponents):
    return (1.0 - ewma_rate) ** np.asarray(exponents, np.float64)


def taps():
    return (ewma_rate * powers(np.arange(BLOCK))).astype(ml_dtypes.bfloat16)


def closing_kernel(rows, x_hbm, weights_hbm, close_ref, ends_ref, x_ref, tail_ref, sems):
    series, width = x_ref.shape
    blocks = width // BLOCK
    steps = series // rows
    ready = pltpu.make_async_copy(weights_hbm.at[:, BLOCK:], tail_ref, sems.at[steps])
    ready.start()
    copies = []
    for i in range(steps):
        at = slice(i * rows, (i + 1) * rows)
        copies.append(pltpu.make_async_copy(x_hbm.at[at], x_ref.at[at], sems.at[i]))
        copies[-1].start()
    block_keep = jnp.float32(powers(BLOCK))
    tile = (LANES, LANES)
    diagonal = lax.broadcasted_iota(jnp.int32, tile, 0) == lax.broadcasted_iota(jnp.int32, tile, 1)
    ready.wait()
    tail = tail_ref[...]
    for i in range(steps):
        at = slice(i * rows, (i + 1) * rows)
        copies[i].wait()
        level = None
        for b in range(blocks):
            end = jnp.dot(
                x_ref[at, b * BLOCK : (b + 1) * BLOCK], tail, preferred_element_type=jnp.float32
            )
            level = end if level is None else end + block_keep * level
            if b + 1 < blocks:
                ends_ref[b, at] = level
        for first in range(0, rows, LANES):
            line = jnp.sum(jnp.where(diagonal, level[first : first + LANES], 0.0), axis=0, keepdims=True)
            close_ref[:, :, i * rows + first : i * rows + first + LANES] = jnp.broadcast_to(
                line[None], (close_ref.shape[0], 1, LANES)
            )


def residual_kernel(
    shards, x_ref, ends_ref, ut_ref, closes_ref, start_ref, weights_ref, step_ref, out_ref, scores_ref
):
    series, width = x_ref.shape
    place = lax.axis_index("tm")

    def weight(table):
        value = jnp.float32(table[0])
        for p in range(1, shards):
            value = jnp.where(place == p, jnp.float32(table[p]), value)
        return value

    line = start_ref[...] * weight([powers(width * p) for p in range(shards)])
    for s in range(shards - 1):
        line += closes_ref[s] * weight(
            [powers(width * (p - 1 - s)) if s < p else 0.0 for p in range(shards)]
        )
    basis = ut_ref[...]
    gram = lax.dot_general(basis, basis, (((1,), (1,)), ((), ())), preferred_element_type=jnp.float32)
    entry = jnp.transpose(jnp.broadcast_to(line, (LANES, series)))
    step = step_ref[...]
    squares = []
    for b in range(width // BLOCK):
        cols = slice(b * BLOCK, (b + 1) * BLOCK)
        local = jnp.dot(x_ref[:, cols], weights_ref[:, :BLOCK], preferred_element_type=jnp.float32)
        level = entry if b == 0 else ends_ref[b - 1] + jnp.float32(powers(b * BLOCK)) * entry
        level = jnp.concatenate([level] * (BLOCK // LANES), axis=1)
        residual = (local - level * step).astype(jnp.bfloat16)
        exact = residual.astype(jnp.float32)
        squares.append(jnp.sum(exact * exact, axis=0, keepdims=True))
        scores_ref[:, cols] = jnp.dot(basis, residual, preferred_element_type=jnp.float32)
    square = jnp.concatenate(squares, axis=1)
    pieces, groups = out_ref.shape[:2]
    halves = pieces * LANES // width
    high = K // halves
    per = K // pieces
    for p in range(pieces):
        j, h = divmod(p, halves)
        cols = slice(j * LANES, (j + 1) * LANES)
        for q in range(groups - 1):
            first = h * high + q * SUBLANES
            out_ref[p, q] = scores_ref[first : first + SUBLANES, cols]
        mine = gram[p * per : (p + 1) * per]
        out_ref[p, groups - 1] = jnp.concatenate(
            [
                square[:, cols],
                jnp.concatenate([mine[: per // 2], mine[per // 2 :]], axis=1),
                jnp.zeros((1, LANES), jnp.float32),
            ],
            axis=0,
        )


def energy_kernel(series, in_ref, scores_ref, energy_ref):
    pieces, groups = in_ref.shape[:2]
    width = scores_ref.shape[1]
    halves = pieces * LANES // width
    high = K // halves
    per = K // pieces
    rows = []
    for p in range(pieces):
        packed = in_ref[p, groups - 1, 1 : 1 + per // 2]
        rows += [packed[:, :K], packed[:, K:]]
    gram = jnp.concatenate(rows, axis=0)
    top = gram.astype(jnp.bfloat16)
    rest = gram - top.astype(jnp.float32)
    middle = rest.astype(jnp.bfloat16)
    low = (rest - middle.astype(jnp.float32)).astype(jnp.bfloat16)
    for p in range(pieces):
        j, h = divmod(p, halves)
        cols = slice(j * LANES, (j + 1) * LANES)
        for q in range(groups - 1):
            first = h * high + q * SUBLANES
            scores_ref[first : first + SUBLANES, cols] = in_ref[p, q]
        if h == 0:
            energy_ref[:, cols] = in_ref[p, groups - 1, 0:1]
    scores = scores_ref[...]
    scores_low = scores.astype(jnp.bfloat16)
    spread = jnp.dot(
        jnp.concatenate([top, middle, low], axis=0), scores_low, preferred_element_type=jnp.float32
    )
    spread = spread[0:K] + spread[K : 2 * K] + spread[2 * K :]
    inside = jnp.sum(scores_low.astype(jnp.float32) * (2.0 * scores - spread), axis=0, keepdims=True)
    energy_ref[...] = (energy_ref[...] - inside) * jnp.float32(1.0 / series)


def constants():
    tap = taps()
    lag = np.arange(BLOCK)[None, :] - np.arange(BLOCK)[:, None] - 1
    toeplitz = np.where(lag >= 0, -tap[np.maximum(lag, 0)], tap[0] * 0).astype(tap.dtype)
    toeplitz += np.eye(BLOCK, dtype=tap.dtype)
    tail = np.broadcast_to(tap[::-1, None], (BLOCK, LANES))
    step = powers(np.arange(BLOCK))[None, :].astype(np.float32)
    return jnp.asarray(np.concatenate([toeplitz, tail], axis=1)), jnp.asarray(step)


VMEM = pl.BlockSpec(memory_space=pltpu.VMEM)
HBM = pl.BlockSpec(memory_space=pltpu.HBM)
LIMIT = pltpu.CompilerParams(vmem_limit_bytes=20 * 1024 * 1024)


def call_closing(rows, shards, traffic, weights):
    series, width = traffic.shape
    return pl.pallas_call(
        functools.partial(closing_kernel, rows),
        in_specs=[HBM, HBM],
        out_specs=[VMEM] * 3,
        out_shape=[
            jax.ShapeDtypeStruct((shards, 1, series), jnp.float32),
            pltpu.VMEM((width // BLOCK - 1, series, LANES), jnp.float32),
            pltpu.VMEM((series, width), jnp.bfloat16),
        ],
        scratch_shapes=[
            pltpu.VMEM((BLOCK, LANES), jnp.bfloat16), pltpu.SemaphoreType.DMA((series // rows + 1,))
        ],
        compiler_params=LIMIT,
        name="closing",
    )(
        pltpu.with_memory_space_constraint(traffic, pltpu.HBM),
        pltpu.with_memory_space_constraint(weights, pltpu.HBM),
    )


def call_residual(shards, pieces, kept, ends, basis, closes, start, weights, step):
    width = kept.shape[1]
    groups = K * width // (pieces * LANES * SUBLANES) + 1
    return pl.pallas_call(
        functools.partial(residual_kernel, shards),
        in_specs=[VMEM] * 7,
        out_specs=VMEM,
        out_shape=jax.ShapeDtypeStruct((pieces, groups, SUBLANES, LANES), jnp.float32),
        scratch_shapes=[pltpu.VMEM((K, width), jnp.float32)],
        compiler_params=LIMIT,
        name="residuals",
    )(kept, ends, basis, closes, start, weights, step)


def call_energy(total, width, every):
    return pl.pallas_call(
        functools.partial(energy_kernel, total),
        in_specs=[VMEM],
        out_specs=[VMEM, VMEM],
        out_shape=[
            jax.ShapeDtypeStruct((K, width), jnp.float32),
            jax.ShapeDtypeStruct((1, width), jnp.float32),
        ],
        name="energies",
    )(pltpu.with_memory_space_constraint(every, pltpu.VMEM))

ROWS = 512
GROUP = ("x", "near", "core")


def shards_fn(shards, total, traffic, start_level, subspace):
    series, width = traffic.shape
    pieces = 1
    for axis in GROUP:
        pieces *= lax.axis_size(axis)
    weights, step = constants()
    close, ends, kept = call_closing(ROWS, shards, traffic, weights)
    closes = lax.all_to_all(close, "tm", 0, 0, tiled=True)
    part = call_residual(
        shards, pieces, kept, ends, subspace.T, closes, start_level.reshape(1, series), weights, step
    )
    mine = jnp.sum(lax.all_to_all(part, GROUP, 0, 0, tiled=True), axis=0)
    far = lax.axis_size("far")
    mine = jnp.sum(
        lax.all_to_all(jnp.broadcast_to(mine[None], (far,) + mine.shape), "far", 0, 0, tiled=True), axis=0
    )
    every = lax.all_to_all(
        jnp.broadcast_to(mine[None], (pieces,) + mine.shape), GROUP, 0, 0, tiled=True
    )
    scores, energy = call_energy(total, width, every)
    return scores, energy.reshape(width)


def solution(mesh):
    times = mesh.shape["tm"]
    fine = Mesh(mesh.devices.reshape(times, 4, 8, 2, 2), ("tm", "x", "far", "near", "core"))
    prefix = ("x", "far", "near", "core")

    def program(traffic, start_level, subspace):
        return jax.shard_map(
            functools.partial(shards_fn, times, traffic.shape[0]),
            mesh=fine,
            in_specs=(P(prefix, "tm"), P(prefix), P(prefix, None)),
            out_specs=(P(None, "tm"), P("tm")),
            check_vma=False,
        )(traffic, start_level, subspace)

    return program
```

time: 705 us -> 73.9 us (0.10)
  waiting for transfers between devices: 328 us -> 0 us
  blocking collectives: 266 us -> 65.6 us
  local copies, waits for them, and re-layouts: 48.7 us -> 0.08 us
  other arithmetic: 26 us -> 0.1 us
  matrix products: 17.5 us -> 0 us
  between operations: 14.1 us -> 0.7 us
  Pallas kernels: 0 us -> 7.15 us
    psum x1 -> x0, waiting for transfers between devices: 328 us -> none  [shards(): scores = lax.psum(local_scores, 'prefix')]
    psum x1 -> x0, blocking collectives: 248 us -> none  [shards(): lax.psum(jnp.sum(remainder * remainder, axis=0), 'prefix') / series_total]
    all_to_all x0 -> x4, blocking collectives: none -> 65.6 us  [the longest x1 27.1 us: shards_fn(): lax.all_to_all(jnp.broadcast_to(mine[None], (far,) + mine.shape), 'far',...]
    reshape x4 -> x0, local copies, waits for them, and re-layouts: 28 us -> none  [the longest x2 14.1 us: shards(): (flat_blocks.astype(jnp.float32) - previous).astype(jnp.bfloat16)]
    dot_general x1 -> x0, other arithmetic: 22.6 us -> none  [shards(): jnp.dot(flat_blocks, tail_weights, preferred_element_type=jnp.float32)]
    dot_general x5 -> x0, matrix products: 17.5 us -> none  [the longest x1 8.02 us: shards(): jnp.dot(flat_blocks, strict_qp, preferred_element_type=jnp.float32)]
    all_gather x1 -> x0, blocking collectives: 10.4 us -> none  [entering(): everything = jax.tree.map(lambda part: lax.all_gather(part, axis), x)]
    unnamed x1 -> x0, blocking collectives: 8.39 us -> none
  transfers between devices with their start and end apart: 1 -> 0, of which waited for: 1 -> 0; matrix products, arithmetic and copies ran while one was open for 1% -> 0% of each run, Pallas kernels for 0% -> 0%
where the time goes in v3:
time: 73.9 us; the launch traced here: 73.7 us
  blocking collectives  65.6 us (89%)
  Pallas kernels  7.15 us (10%)
    all_to_all x1, blocking collectives, shards_fn(): lax.all_to_all(jnp.broadcast_to(mine[None], (far,) + mine.shape), 'far',...  27.1 us
    all_to_all x1, blocking collectives, shards_fn(): mine = jnp.sum(lax.all_to_all(part, GROUP, 0, 0, tiled=True), axis=0)  15.4 us
    all_to_all x1, blocking collectives, shards_fn(): lax.all_to_all(jnp.broadcast_to(mine[None], (pieces,) + mine.shape), GROU...  14 us
    all_to_all x1, blocking collectives, shards_fn(): closes = lax.all_to_all(close, 'tm', 0, 0, tiled=True)  9.11 us
    pallas_call x1, Pallas kernels, call_closing(): pl.pallas_call(functools.partial(closing_kernel, rows), in_specs=[HBM, HB...  3.18 us
    pallas_call x1, Pallas kernels, call_residual(): pl.pallas_call(functools.partial(residual_kernel, shards), in_specs=[VMEM...  3.02 us

profile of v3, /device:TPU:1, one launch (start us, length us, event | category | flops | bytes accessed | tf_op | source)
XLA Modules:
  0.0 73.7 jit_solution(4355665617241957885)
XLA Ops:
  0.6 0.0 copy-start
  0.6 0.0 copy-start.3
  0.7 0.0 copy-start.1
  0.7 0.0 copy-start.2
  0.7 3.2 %closing.1 = (f32[4,1,2048]{2,1,0:T(1,128)S(1)}, f32[3,2048,128]{2,1,0:T(8,128)S(1)}, bf16[2048,1024]{1,0:T(8,128)(2,1)S(1)}) custom-call(bf16[2048,1024]{1,0:T(8,128)(2,1)} %x_hbm.1, bf16[256,384]{1,0:T(8,128)(2,1)} %constant.6.clone.weights_hbm.weights_ref), custom_call_target="tpu_custom_call" | custom-call | tf_op jit(solution)/shard_map/closing/pallas_call | solution.py:164
  3.9 9.1 %all_to_all.20.closes_ref = f32[4,1,2048]{2,1,0:T(1,128)S(1)} all-to-all(f32[4,1,2048]{2,1,0:T(1,128)S(1)} %get-tuple-element.9), channel_id=1, replica_groups=mesh['tm'=4,'x'=4,'far'=8,'near'=2,'core'=2] {'tm'}, dimensions={0} | all-to-all | bytes 65536 | tf_op jit(solution)/shard_map/all_to_all | solution.py:221
  13.0 0.0 copy-done
  13.0 0.0 copy-done.3
  13.0 0.0 copy-done.1
  13.0 0.0 copy-done.2
  13.0 3.0 %residuals.1 = f32[16,9,4,128]{3,2,1,0:T(4,128)S(1)} custom-call(bf16[2048,1024]{1,0:T(8,128)(2,1)S(1)} %get-tuple-element.7.x_ref, f32[3,2048,128]{2,1,0:T(8,128)S(1)} %get-tuple-element.8.ends_ref, bf16[64,2048]{1,0:T(8,128)(2,1)S(1)} %bitcast.3, f32[4,1,2048]{2,1,0:T(1,128)S(1)} %all_to_all.20.closes_ref, f32[1,2048]{1,0:T(1,128)S(1)} %bitcast.4, ...), custom_call_target="tpu_custom_call" | custom-call | tf_op jit(solution)/shard_map/residuals/pallas_call | solution.py:187
  16.0 15.4 %all_to_all.21 = f32[16,9,4,128]{3,2,1,0:T(4,128)S(1)} all-to-all(f32[16,9,4,128]{3,2,1,0:T(4,128)S(1)} %residuals.1), channel_id=1, replica_groups=mesh['tm'=4,'x'=4,'far'=8,'near'=2,'core'=2] {'x','near','core'}, dimensions={0} | all-to-all | bytes 589824 | tf_op jit(solution)/shard_map/all_to_all | solution.py:225
  31.5 0.1 reduce_sum.18
  31.5 27.1 %all_to_all.22 = f32[8,9,4,128]{3,2,1,0:T(4,128)S(1)} all-to-all(f32[8,9,4,128]{3,2,1,0:T(4,128)S(1)} %broadcast_in_dim.4), channel_id=1, replica_groups=mesh['tm'=4,'x'=4,'far'=8,'near'=2,'core'=2] {'far'}, dimensions={0} | all-to-all | bytes 294912 | tf_op jit(solution)/shard_map/all_to_all | solution.py:228
  58.8 14.0 %all_to_all.23.in_ref = f32[16,9,4,128]{3,2,1,0:T(4,128)S(1)} all-to-all(f32[16,9,4,128]{3,2,1,0:T(4,128)S(1)} %broadcast_in_dim.5), channel_id=1, replica_groups=mesh['tm'=4,'x'=4,'far'=8,'near'=2,'core'=2] {'x','near','core'}, dimensions={0} | all-to-all | bytes 589824 | tf_op jit(solution)/shard_map/all_to_all | solution.py:230
  72.7 1.0 %energies.1 = (f32[64,1024]{1,0:T(8,128)}, f32[1,1024]{1,0:T(1,128)}) custom-call(f32[16,9,4,128]{3,2,1,0:T(4,128)S(1)} %all_to_all.23.in_ref), custom_call_target="tpu_custom_call" | custom-call | tf_op jit(solution)/shard_map/energies/pallas_call | solution.py:199
  (3 shorter events, 0.1 us)
Async XLA Ops:
  0.6 12.4 %copy-start = (bf16[256,384]{1,0:T(8,128)(2,1)S(1)}, bf16[256,384]{1,0:T(8,128)(2,1)}, u32[]{:S(2)}) copy-start(bf16[256,384]{1,0:T(8,128)(2,1)} %constant.6.clone.weights_hbm.weights_ref) | copy-start | bytes 589828
  0.6 12.3 %copy-start.3 = (f32[1,256]{1,0:T(1,128)S(1)}, f32[1,256]{1,0:T(1,128)}, u32[]{:S(2)}) copy-start(f32[1,256]{1,0:T(1,128)} %constant.7.clone.step_ref) | copy-start | bytes 3076
  0.7 12.3 %copy-start.1 = (bf16[2048,64]{0,1:T(8,128)(2,1)S(1)}, bf16[2048,64]{0,1:T(8,128)(2,1)}, u32[]{:S(2)}) copy-start(bf16[2048,64]{0,1:T(8,128)(2,1)} %param.7) | copy-start | bytes 786436
  0.7 12.3 %copy-start.2 = (f32[2048]{0:T(1024)S(1)}, f32[2048]{0:T(1024)}, u32[]{:S(2)}) copy-start(f32[2048]{0:T(1024)} %param.6) | copy-start | bytes 24580

commit v4 on v3

--- a/solution.py
+++ b/solution.py
@@ -210,6 +210,17 @@
 ROWS = 512
 GROUP = ("x", "near", "core")
 
+NEAR_FIRST = 11
+FAR_FIRST = 5
+
+
+def order(size, first):
+    return [[(first + i) % size for i in range(size)]]
+
+
+def exchange(x, axes, groups):
+    return lax.all_to_all(x, axes, 0, 0, axis_index_groups=groups, tiled=True)
+
 
 def shards_fn(shards, total, traffic, start_level, subspace):
     series, width = traffic.shape
@@ -222,14 +233,13 @@
     part = call_residual(
         shards, pieces, kept, ends, subspace.T, closes, start_level.reshape(1, series), weights, step
     )
-    mine = jnp.sum(lax.all_to_all(part, GROUP, 0, 0, tiled=True), axis=0)
+    near = order(pieces, NEAR_FIRST)
     far = lax.axis_size("far")
+    mine = jnp.sum(exchange(part, GROUP, near), axis=0)
     mine = jnp.sum(
-        lax.all_to_all(jnp.broadcast_to(mine[None], (far,) + mine.shape), "far", 0, 0, tiled=True), axis=0
-    )
-    every = lax.all_to_all(
-        jnp.broadcast_to(mine[None], (pieces,) + mine.shape), GROUP, 0, 0, tiled=True
-    )
+        exchange(jnp.broadcast_to(mine[None], (far,) + mine.shape), "far", order(far, FAR_FIRST)), axis=0
+    )
+    every = exchange(jnp.broadcast_to(mine[None], (pieces,) + mine.shape), GROUP, near)
     scores, energy = call_energy(total, width, every)
     return scores, energy.reshape(width)
 

time: 73.9 us -> 65.5 us (0.89)
  blocking collectives: 65.6 us -> 57.2 us
    all_to_all x3, blocking collectives: 56.5 us -> 48.1 us  [exchange(): return lax.all_to_all(x, axes, 0, 0, axis_index_groups=groups, tiled=True)]
where the time goes in v4:
time: 65.5 us; the launch traced here: 65.3 us
  blocking collectives  57.2 us (87%)
  Pallas kernels  7.15 us (11%)
  between operations  0.7 us (1%)
    all_to_all x3, blocking collectives, exchange(): return lax.all_to_all(x, axes, 0, 0, axis_index_groups=groups, tiled=True)  48.1 us
    all_to_all x1, blocking collectives, shards_fn(): closes = lax.all_to_all(close, 'tm', 0, 0, tiled=True)  9.11 us
    pallas_call x1, Pallas kernels, call_closing(): pl.pallas_call(functools.partial(closing_kernel, rows), in_specs=[HBM, HB...  3.18 us
    pallas_call x1, Pallas kernels, call_residual(): pl.pallas_call(functools.partial(residual_kernel, shards), in_specs=[VMEM...  3.02 us

profile of v4, /device:TPU:1, one launch (start us, length us, event | category | flops | bytes accessed | tf_op | source)
XLA Modules:
  0.0 65.3 jit_solution(17725134837751635152)
XLA Ops:
  0.6 0.0 copy-start
  0.6 0.0 copy-start.3
  0.7 0.0 copy-start.1
  0.7 0.0 copy-start.2
  0.7 3.2 %closing.1 = (f32[4,1,2048]{2,1,0:T(1,128)S(1)}, f32[3,2048,128]{2,1,0:T(8,128)S(1)}, bf16[2048,1024]{1,0:T(8,128)(2,1)S(1)}) custom-call(bf16[2048,1024]{1,0:T(8,128)(2,1)} %x_hbm.1, bf16[256,384]{1,0:T(8,128)(2,1)} %constant.6.clone.weights_hbm.weights_ref), custom_call_target="tpu_custom_call" | custom-call | tf_op jit(solution)/shard_map/closing/pallas_call | solution.py:164
  3.9 9.1 %all_to_all.20.closes_ref = f32[4,1,2048]{2,1,0:T(1,128)S(1)} all-to-all(f32[4,1,2048]{2,1,0:T(1,128)S(1)} %get-tuple-element.9), channel_id=1, replica_groups=mesh['tm'=4,'x'=4,'far'=8,'near'=2,'core'=2] {'tm'}, dimensions={0} | all-to-all | bytes 65536 | tf_op jit(solution)/shard_map/all_to_all | solution.py:232
  13.0 0.0 copy-done
  13.0 0.0 copy-done.3
  13.0 0.0 copy-done.1
  13.0 0.0 copy-done.2
  13.0 3.0 %residuals.1 = f32[16,9,4,128]{3,2,1,0:T(4,128)S(1)} custom-call(bf16[2048,1024]{1,0:T(8,128)(2,1)S(1)} %get-tuple-element.7.x_ref, f32[3,2048,128]{2,1,0:T(8,128)S(1)} %get-tuple-element.8.ends_ref, bf16[64,2048]{1,0:T(8,128)(2,1)S(1)} %bitcast.3, f32[4,1,2048]{2,1,0:T(1,128)S(1)} %all_to_all.20.closes_ref, f32[1,2048]{1,0:T(1,128)S(1)} %bitcast.4, ...), custom_call_target="tpu_custom_call" | custom-call | tf_op jit(solution)/shard_map/residuals/pallas_call | solution.py:187
  16.0 15.1 %all_to_all.21 = f32[16,9,4,128]{3,2,1,0:T(4,128)S(1)} all-to-all(f32[16,9,4,128]{3,2,1,0:T(4,128)S(1)} %residuals.1), channel_id=1, replica_groups={{67,96,97,98,99,0,1,2,3,32,33,34,35,64,65,66},{71,100,101,102,103,4,5,6..., dimensions={0} | all-to-all | bytes 589824 | tf_op jit(solution)/shard_map/all_to_all | solution.py:222
  31.2 0.1 reduce_sum.18
  31.2 20.9 %all_to_all.22 = f32[8,9,4,128]{3,2,1,0:T(4,128)S(1)} all-to-all(f32[8,9,4,128]{3,2,1,0:T(4,128)S(1)} %broadcast_in_dim.4), channel_id=1, replica_groups={{20,24,28,0,4,8,12,16},{21,25,29,1,5,9,13,17},{22,26,30,2,6,10,14,18},{..., dimensions={0} | all-to-all | bytes 294912 | tf_op jit(solution)/shard_map/all_to_all | solution.py:222
  52.3 12.0 %all_to_all.23.in_ref = f32[16,9,4,128]{3,2,1,0:T(4,128)S(1)} all-to-all(f32[16,9,4,128]{3,2,1,0:T(4,128)S(1)} %broadcast_in_dim.5), channel_id=1, replica_groups={{67,96,97,98,99,0,1,2,3,32,33,34,35,64,65,66},{71,100,101,102,103,4,5,6..., dimensions={0} | all-to-all | bytes 589824 | tf_op jit(solution)/shard_map/all_to_all | solution.py:222
  64.3 1.0 %energies.1 = (f32[64,1024]{1,0:T(8,128)}, f32[1,1024]{1,0:T(1,128)}) custom-call(f32[16,9,4,128]{3,2,1,0:T(4,128)S(1)} %all_to_all.23.in_ref), custom_call_target="tpu_custom_call" | custom-call | tf_op jit(solution)/shard_map/energies/pallas_call | solution.py:199
  (3 shorter events, 0.1 us)
Async XLA Ops:
  0.6 12.4 %copy-start = (bf16[256,384]{1,0:T(8,128)(2,1)S(1)}, bf16[256,384]{1,0:T(8,128)(2,1)}, u32[]{:S(2)}) copy-start(bf16[256,384]{1,0:T(8,128)(2,1)} %constant.6.clone.weights_hbm.weights_ref) | copy-start | bytes 589828
  0.6 12.3 %copy-start.3 = (f32[1,256]{1,0:T(1,128)S(1)}, f32[1,256]{1,0:T(1,128)}, u32[]{:S(2)}) copy-start(f32[1,256]{1,0:T(1,128)} %constant.7.clone.step_ref) | copy-start | bytes 3076
  0.7 12.3 %copy-start.1 = (bf16[2048,64]{0,1:T(8,128)(2,1)S(1)}, bf16[2048,64]{0,1:T(8,128)(2,1)}, u32[]{:S(2)}) copy-start(bf16[2048,64]{0,1:T(8,128)(2,1)} %param.7) | copy-start | bytes 786436
  0.7 12.3 %copy-start.2 = (f32[2048]{0:T(1024)S(1)}, f32[2048]{0:T(1024)}, u32[]{:S(2)}) copy-start(f32[2048]{0:T(1024)} %param.6) | copy-start | bytes 24580

commit v5 on v3

--- a/solution.py
+++ b/solution.py
@@ -7,7 +7,7 @@
 from jax import lax
 from jax.experimental import pallas as pl
 from jax.experimental.pallas import tpu as pltpu
-from jax.sharding import Mesh, PartitionSpec as P
+from jax.sharding import PartitionSpec as P
 
 BLOCK = 256
 LANES = 128
@@ -72,7 +72,7 @@
 
     line = start_ref[...] * weight([powers(width * p) for p in range(shards)])
     for s in range(shards - 1):
-        line += closes_ref[s] * weight(
+        line += closes_ref[(s - TIME_FIRST) % shards] * weight(
             [powers(width * (p - 1 - s)) if s < p else 0.0 for p in range(shards)]
         )
     basis = ut_ref[...]
@@ -208,42 +208,64 @@
     )(pltpu.with_memory_space_constraint(every, pltpu.VMEM))
 
 ROWS = 512
-GROUP = ("x", "near", "core")
+
+NEAR_FIRST = 11
+FAR_FIRST = 5
+TIME_FIRST = 2
+
+
+def rotated(items, first):
+    items = list(items)
+    return items[first:] + items[:first]
+
+
+def stages(x_size, z_size, cores):
+    pairs = z_size // 2
+
+    def device(x, pair, which, core):
+        z = 2 * pair + (which if pair < pairs // 2 else 1 - which)
+        return (x * z_size + z) * cores + core
+
+    places = [(x, which, core) for x in range(x_size) for which in range(2) for core in range(cores)]
+    near = [
+        [device(x, pair, which, core) for x, which, core in rotated(places, NEAR_FIRST)]
+        for pair in range(pairs)
+    ]
+    far = [
+        [device(x, pair, which, core) for pair in rotated(range(pairs), FAR_FIRST)]
+        for x, which, core in places
+    ]
+    return near, far
+
+
+def exchange(x, axis, groups):
+    return lax.all_to_all(x, axis, 0, 0, axis_index_groups=groups, tiled=True)
 
 
 def shards_fn(shards, total, traffic, start_level, subspace):
     series, width = traffic.shape
-    pieces = 1
-    for axis in GROUP:
-        pieces *= lax.axis_size(axis)
+    near, far = stages(4, 16, 2)
+    pieces = len(near[0])
     weights, step = constants()
     close, ends, kept = call_closing(ROWS, shards, traffic, weights)
-    closes = lax.all_to_all(close, "tm", 0, 0, tiled=True)
+    closes = exchange(close, "tm", [rotated(range(shards), TIME_FIRST)])
     part = call_residual(
         shards, pieces, kept, ends, subspace.T, closes, start_level.reshape(1, series), weights, step
     )
-    mine = jnp.sum(lax.all_to_all(part, GROUP, 0, 0, tiled=True), axis=0)
-    far = lax.axis_size("far")
-    mine = jnp.sum(
-        lax.all_to_all(jnp.broadcast_to(mine[None], (far,) + mine.shape), "far", 0, 0, tiled=True), axis=0
-    )
-    every = lax.all_to_all(
-        jnp.broadcast_to(mine[None], (pieces,) + mine.shape), GROUP, 0, 0, tiled=True
-    )
+    mine = jnp.sum(exchange(part, "prefix", near), axis=0)
+    mine = jnp.broadcast_to(mine[None], (len(far[0]),) + mine.shape)
+    mine = jnp.sum(exchange(mine, "prefix", far), axis=0)
+    every = exchange(jnp.broadcast_to(mine[None], (pieces,) + mine.shape), "prefix", near)
     scores, energy = call_energy(total, width, every)
     return scores, energy.reshape(width)
 
 
 def solution(mesh):
-    times = mesh.shape["tm"]
-    fine = Mesh(mesh.devices.reshape(times, 4, 8, 2, 2), ("tm", "x", "far", "near", "core"))
-    prefix = ("x", "far", "near", "core")
-
     def program(traffic, start_level, subspace):
         return jax.shard_map(
-            functools.partial(shards_fn, times, traffic.shape[0]),
-            mesh=fine,
-            in_specs=(P(prefix, "tm"), P(prefix), P(prefix, None)),
+            functools.partial(shards_fn, mesh.shape["tm"], traffic.shape[0]),
+            mesh=mesh,
+            in_specs=(P("prefix", "tm"), P("prefix"), P("prefix", None)),
             out_specs=(P(None, "tm"), P("tm")),
             check_vma=False,
         )(traffic, start_level, subspace)

time: 73.9 us -> 63.8 us (0.86)
  blocking collectives: 65.6 us -> 55.5 us
    all_to_all x4, blocking collectives: 65.6 us -> 55.5 us  [exchange(): return lax.all_to_all(x, axis, 0, 0, axis_index_groups=groups, tiled=True)]
where the time goes in v5:
time: 63.8 us; the launch traced here: 63.5 us
  blocking collectives  55.5 us (87%)
  Pallas kernels  7.15 us (11%)
  between operations  0.7 us (1%)
    all_to_all x4, blocking collectives, exchange(): return lax.all_to_all(x, axis, 0, 0, axis_index_groups=groups, tiled=True)  55.5 us
    pallas_call x1, Pallas kernels, call_closing(): pl.pallas_call(functools.partial(closing_kernel, rows), in_specs=[HBM, HB...  3.18 us
    pallas_call x1, Pallas kernels, call_residual(): pl.pallas_call(functools.partial(residual_kernel, shards), in_specs=[VMEM...  3.02 us

profile of v5, /device:TPU:1, one launch (start us, length us, event | category | flops | bytes accessed | tf_op | source)
XLA Modules:
  0.0 63.5 jit_solution(987881192878052888)
XLA Ops:
  0.6 0.0 copy-start
  0.6 0.0 copy-start.3
  0.7 0.0 copy-start.1
  0.7 0.0 copy-start.2
  0.7 3.2 %closing.1 = (f32[4,1,2048]{2,1,0:T(1,128)S(1)}, f32[3,2048,128]{2,1,0:T(8,128)S(1)}, bf16[2048,1024]{1,0:T(8,128)(2,1)S(1)}) custom-call(bf16[2048,1024]{1,0:T(8,128)(2,1)} %x_hbm.1, bf16[256,384]{1,0:T(8,128)(2,1)} %constant.6.clone.weights_hbm.weights_ref), custom_call_target="tpu_custom_call" | custom-call | tf_op jit(solution)/shard_map/closing/pallas_call | solution.py:164
  3.9 7.6 %all_to_all.20.closes_ref = f32[4,1,2048]{2,1,0:T(1,128)S(1)} all-to-all(f32[4,1,2048]{2,1,0:T(1,128)S(1)} %get-tuple-element.9), channel_id=1, replica_groups={{256,384,0,128},{257,385,1,129},{258,386,2,130},{259,387,3,131},{260,38..., dimensions={0} | all-to-all | bytes 65536 | tf_op jit(solution)/shard_map/all_to_all | solution.py:242
  11.5 0.0 copy-done
  11.5 0.0 copy-done.3
  11.5 0.0 copy-done.1
  11.5 0.0 copy-done.2
  11.5 3.0 %residuals.1 = f32[16,9,4,128]{3,2,1,0:T(4,128)S(1)} custom-call(bf16[2048,1024]{1,0:T(8,128)(2,1)S(1)} %get-tuple-element.7.x_ref, f32[3,2048,128]{2,1,0:T(8,128)S(1)} %get-tuple-element.8.ends_ref, bf16[64,2048]{1,0:T(8,128)(2,1)S(1)} %bitcast.3, f32[4,1,2048]{2,1,0:T(1,128)S(1)} %all_to_all.20.closes_ref, f32[1,2048]{1,0:T(1,128)S(1)} %bitcast.4, ...), custom_call_target="tpu_custom_call" | custom-call | tf_op jit(solution)/shard_map/residuals/pallas_call | solution.py:187
  14.5 15.8 %all_to_all.21 = f32[16,9,4,128]{3,2,1,0:T(4,128)S(1)} all-to-all(f32[16,9,4,128]{3,2,1,0:T(4,128)S(1)} %residuals.1), channel_id=1, replica_groups={{67,96,97,98,99,0,1,2,3,32,33,34,35,64,65,66},{71,100,101,102,103,4,5,6..., dimensions={0} | all-to-all | bytes 589824 | tf_op jit(solution)/shard_map/all_to_all | solution.py:242
  30.4 0.1 reduce_sum.18
  30.4 18.4 %all_to_all.22 = f32[8,9,4,128]{3,2,1,0:T(4,128)S(1)} all-to-all(f32[8,9,4,128]{3,2,1,0:T(4,128)S(1)} %broadcast_in_dim.4), channel_id=1, replica_groups={{22,26,30,0,4,8,12,18},{23,27,31,1,5,9,13,19},{20,24,28,2,6,10,14,16},{..., dimensions={0} | all-to-all | bytes 294912 | tf_op jit(solution)/shard_map/all_to_all | solution.py:242
  48.9 13.6 %all_to_all.23.in_ref = f32[16,9,4,128]{3,2,1,0:T(4,128)S(1)} all-to-all(f32[16,9,4,128]{3,2,1,0:T(4,128)S(1)} %broadcast_in_dim.5), channel_id=1, replica_groups={{67,96,97,98,99,0,1,2,3,32,33,34,35,64,65,66},{71,100,101,102,103,4,5,6..., dimensions={0} | all-to-all | bytes 589824 | tf_op jit(solution)/shard_map/all_to_all | solution.py:242
  62.6 1.0 %energies.1 = (f32[64,1024]{1,0:T(8,128)}, f32[1,1024]{1,0:T(1,128)}) custom-call(f32[16,9,4,128]{3,2,1,0:T(4,128)S(1)} %all_to_all.23.in_ref), custom_call_target="tpu_custom_call" | custom-call | tf_op jit(solution)/shard_map/energies/pallas_call | solution.py:199
  (3 shorter events, 0.1 us)
Async XLA Ops:
  0.6 10.9 %copy-start = (bf16[256,384]{1,0:T(8,128)(2,1)S(1)}, bf16[256,384]{1,0:T(8,128)(2,1)}, u32[]{:S(2)}) copy-start(bf16[256,384]{1,0:T(8,128)(2,1)} %constant.6.clone.weights_hbm.weights_ref) | copy-start | bytes 589828
  0.6 10.8 %copy-start.3 = (f32[1,256]{1,0:T(1,128)S(1)}, f32[1,256]{1,0:T(1,128)}, u32[]{:S(2)}) copy-start(f32[1,256]{1,0:T(1,128)} %constant.7.clone.step_ref) | copy-start | bytes 3076
  0.7 10.8 %copy-start.1 = (bf16[2048,64]{0,1:T(8,128)(2,1)S(1)}, bf16[2048,64]{0,1:T(8,128)(2,1)}, u32[]{:S(2)}) copy-start(bf16[2048,64]{0,1:T(8,128)(2,1)} %param.7) | copy-start | bytes 786436
  0.7 10.8 %copy-start.2 = (f32[2048]{0:T(1024)S(1)}, f32[2048]{0:T(1024)}, u32[]{:S(2)}) copy-start(f32[2048]{0:T(1024)} %param.6) | copy-start | bytes 24580

commit v6 on v5

--- a/solution.py
+++ b/solution.py
@@ -80,6 +80,7 @@
     entry = jnp.transpose(jnp.broadcast_to(line, (LANES, series)))
     step = step_ref[...]
     squares = []
+    residuals = []
     for b in range(width // BLOCK):
         cols = slice(b * BLOCK, (b + 1) * BLOCK)
         local = jnp.dot(x_ref[:, cols], weights_ref[:, :BLOCK], preferred_element_type=jnp.float32)
@@ -88,7 +89,11 @@
         residual = (local - level * step).astype(jnp.bfloat16)
         exact = residual.astype(jnp.float32)
         squares.append(jnp.sum(exact * exact, axis=0, keepdims=True))
-        scores_ref[:, cols] = jnp.dot(basis, residual, preferred_element_type=jnp.float32)
+        residuals.append(residual)
+    for b in range(width // BLOCK):
+        scores_ref[:, b * BLOCK : (b + 1) * BLOCK] = jnp.dot(
+            basis, residuals[b], preferred_element_type=jnp.float32
+        )
     square = jnp.concatenate(squares, axis=1)
     pieces, groups = out_ref.shape[:2]
     halves = pieces * LANES // width
@@ -210,7 +215,7 @@
 ROWS = 512
 
 NEAR_FIRST = 11
-FAR_FIRST = 5
+FAR = (5, 0, 2, 7, 1, 6, 3, 4)
 TIME_FIRST = 2
 
 
@@ -232,7 +237,7 @@
         for pair in range(pairs)
     ]
     far = [
-        [device(x, pair, which, core) for pair in rotated(range(pairs), FAR_FIRST)]
+        [device(x, pair, which, core) for pair in FAR]
         for x, which, core in places
     ]
     return near, far

time: 63.8 us -> 62.2 us (0.975)
  blocking collectives: 55.5 us -> 54.2 us
    all_to_all x4, blocking collectives: 55.5 us -> 54.2 us  [exchange(): return lax.all_to_all(x, axis, 0, 0, axis_index_groups=groups, tiled=True)]
where the time goes in v6:
time: 62.2 us; the launch traced here: 61.9 us
  blocking collectives  54.2 us (87%)
  Pallas kernels  6.82 us (11%)
  between operations  0.7 us (1%)
    all_to_all x4, blocking collectives, exchange(): return lax.all_to_all(x, axis, 0, 0, axis_index_groups=groups, tiled=True)  54.2 us
    pallas_call x1, Pallas kernels, call_closing(): pl.pallas_call(functools.partial(closing_kernel, rows), in_specs=[HBM, HB...  3.18 us
    pallas_call x1, Pallas kernels, call_residual(): pl.pallas_call(functools.partial(residual_kernel, shards), in_specs=[VMEM...  2.69 us

profile of v6, /device:TPU:1, one launch (start us, length us, event | category | flops | bytes accessed | tf_op | source)
XLA Modules:
  0.0 61.9 jit_solution(7266714434586227427)
XLA Ops:
  0.6 0.0 copy-start
  0.6 0.0 copy-start.3
  0.7 0.0 copy-start.1
  0.7 0.0 copy-start.2
  0.7 3.2 %closing.1 = (f32[4,1,2048]{2,1,0:T(1,128)S(1)}, f32[3,2048,128]{2,1,0:T(8,128)S(1)}, bf16[2048,1024]{1,0:T(8,128)(2,1)S(1)}) custom-call(bf16[2048,1024]{1,0:T(8,128)(2,1)} %x_hbm.1, bf16[256,384]{1,0:T(8,128)(2,1)} %constant.6.clone.weights_hbm.weights_ref), custom_call_target="tpu_custom_call" | custom-call | tf_op jit(solution)/shard_map/closing/pallas_call | solution.py:169
  3.9 7.6 %all_to_all.20.closes_ref = f32[4,1,2048]{2,1,0:T(1,128)S(1)} all-to-all(f32[4,1,2048]{2,1,0:T(1,128)S(1)} %get-tuple-element.9), channel_id=1, replica_groups={{256,384,0,128},{257,385,1,129},{258,386,2,130},{259,387,3,131},{260,38..., dimensions={0} | all-to-all | bytes 65536 | tf_op jit(solution)/shard_map/all_to_all | solution.py:247
  11.5 0.0 copy-done
  11.5 0.0 copy-done.3
  11.5 0.0 copy-done.1
  11.5 0.0 copy-done.2
  11.5 2.7 %residuals.1 = f32[16,9,4,128]{3,2,1,0:T(4,128)S(1)} custom-call(bf16[2048,1024]{1,0:T(8,128)(2,1)S(1)} %get-tuple-element.7.x_ref, f32[3,2048,128]{2,1,0:T(8,128)S(1)} %get-tuple-element.8.ends_ref, bf16[64,2048]{1,0:T(8,128)(2,1)S(1)} %bitcast.3, f32[4,1,2048]{2,1,0:T(1,128)S(1)} %all_to_all.20.closes_ref, f32[1,2048]{1,0:T(1,128)S(1)} %bitcast.4, ...), custom_call_target="tpu_custom_call" | custom-call | tf_op jit(solution)/shard_map/residuals/pallas_call | solution.py:192
  14.2 15.8 %all_to_all.21 = f32[16,9,4,128]{3,2,1,0:T(4,128)S(1)} all-to-all(f32[16,9,4,128]{3,2,1,0:T(4,128)S(1)} %residuals.1), channel_id=1, replica_groups={{67,96,97,98,99,0,1,2,3,32,33,34,35,64,65,66},{71,100,101,102,103,4,5,6..., dimensions={0} | all-to-all | bytes 589824 | tf_op jit(solution)/shard_map/all_to_all | solution.py:247
  30.0 0.1 reduce_sum.18
  30.1 19.1 %all_to_all.22 = f32[8,9,4,128]{3,2,1,0:T(4,128)S(1)} all-to-all(f32[8,9,4,128]{3,2,1,0:T(4,128)S(1)} %broadcast_in_dim.4), channel_id=1, replica_groups={{22,0,8,30,4,26,12,18},{23,1,9,31,5,27,13,19},{20,2,10,28,6,24,14,16},{..., dimensions={0} | all-to-all | bytes 294912 | tf_op jit(solution)/shard_map/all_to_all | solution.py:247
  49.3 11.7 %all_to_all.23.in_ref = f32[16,9,4,128]{3,2,1,0:T(4,128)S(1)} all-to-all(f32[16,9,4,128]{3,2,1,0:T(4,128)S(1)} %broadcast_in_dim.5), channel_id=1, replica_groups={{67,96,97,98,99,0,1,2,3,32,33,34,35,64,65,66},{71,100,101,102,103,4,5,6..., dimensions={0} | all-to-all | bytes 589824 | tf_op jit(solution)/shard_map/all_to_all | solution.py:247
  61.0 1.0 %energies.1 = (f32[64,1024]{1,0:T(8,128)}, f32[1,1024]{1,0:T(1,128)}) custom-call(f32[16,9,4,128]{3,2,1,0:T(4,128)S(1)} %all_to_all.23.in_ref), custom_call_target="tpu_custom_call" | custom-call | tf_op jit(solution)/shard_map/energies/pallas_call | solution.py:204
  (3 shorter events, 0.1 us)
Async XLA Ops:
  0.6 10.9 %copy-start = (bf16[256,384]{1,0:T(8,128)(2,1)S(1)}, bf16[256,384]{1,0:T(8,128)(2,1)}, u32[]{:S(2)}) copy-start(bf16[256,384]{1,0:T(8,128)(2,1)} %constant.6.clone.weights_hbm.weights_ref) | copy-start | bytes 589828
  0.6 10.8 %copy-start.3 = (f32[1,256]{1,0:T(1,128)S(1)}, f32[1,256]{1,0:T(1,128)}, u32[]{:S(2)}) copy-start(f32[1,256]{1,0:T(1,128)} %constant.7.clone.step_ref) | copy-start | bytes 3076
  0.7 10.8 %copy-start.1 = (bf16[2048,64]{0,1:T(8,128)(2,1)S(1)}, bf16[2048,64]{0,1:T(8,128)(2,1)}, u32[]{:S(2)}) copy-start(bf16[2048,64]{0,1:T(8,128)(2,1)} %param.7) | copy-start | bytes 786436
  0.7 10.8 %copy-start.2 = (f32[2048]{0:T(1024)S(1)}, f32[2048]{0:T(1024)}, u32[]{:S(2)}) copy-start(f32[2048]{0:T(1024)} %param.6) | copy-start | bytes 24580

commit v7 on v6

--- a/solution.py
+++ b/solution.py
@@ -214,8 +214,8 @@
 
 ROWS = 512
 
-NEAR_FIRST = 11
-FAR = (5, 0, 2, 7, 1, 6, 3, 4)
+NEAR = (11, 9, 10, 8, 3, 1, 2, 0, 7, 5, 6, 4, 15, 13, 14, 12)
+FAR = (5, 0, 2, 1, 7, 6, 3, 4)
 TIME_FIRST = 2
 
 
@@ -233,7 +233,7 @@
 
     places = [(x, which, core) for x in range(x_size) for which in range(2) for core in range(cores)]
     near = [
-        [device(x, pair, which, core) for x, which, core in rotated(places, NEAR_FIRST)]
+        [device(x, pair, which, core) for x, which, core in [places[i] for i in NEAR]]
         for pair in range(pairs)
     ]
     far = [

time: 62.2 us -> 61.9 us (level)
  no operation moved by 1% of the time
where the time goes in v7:
time: 61.9 us; the launch traced here: 61.7 us
  blocking collectives  54 us (87%)
  Pallas kernels  6.82 us (11%)
  between operations  0.7 us (1%)
    all_to_all x4, blocking collectives, exchange(): return lax.all_to_all(x, axis, 0, 0, axis_index_groups=groups, tiled=True)  54 us
    pallas_call x1, Pallas kernels, call_closing(): pl.pallas_call(functools.partial(closing_kernel, rows), in_specs=[HBM, HB...  3.18 us
    pallas_call x1, Pallas kernels, call_residual(): pl.pallas_call(functools.partial(residual_kernel, shards), in_specs=[VMEM...  2.69 us

profile of v7, /device:TPU:1, one launch (start us, length us, event | category | flops | bytes accessed | tf_op | source)
XLA Modules:
  0.0 61.7 jit_solution(6630017429949758059)
XLA Ops:
  0.6 0.0 copy-start
  0.6 0.0 copy-start.3
  0.7 0.0 copy-start.1
  0.7 0.0 copy-start.2
  0.7 3.2 %closing.1 = (f32[4,1,2048]{2,1,0:T(1,128)S(1)}, f32[3,2048,128]{2,1,0:T(8,128)S(1)}, bf16[2048,1024]{1,0:T(8,128)(2,1)S(1)}) custom-call(bf16[2048,1024]{1,0:T(8,128)(2,1)} %x_hbm.1, bf16[256,384]{1,0:T(8,128)(2,1)} %constant.6.clone.weights_hbm.weights_ref), custom_call_target="tpu_custom_call" | custom-call | tf_op jit(solution)/shard_map/closing/pallas_call | solution.py:169
  3.9 7.6 %all_to_all.20.closes_ref = f32[4,1,2048]{2,1,0:T(1,128)S(1)} all-to-all(f32[4,1,2048]{2,1,0:T(1,128)S(1)} %get-tuple-element.9), channel_id=1, replica_groups={{256,384,0,128},{257,385,1,129},{258,386,2,130},{259,387,3,131},{260,38..., dimensions={0} | all-to-all | bytes 65536 | tf_op jit(solution)/shard_map/all_to_all | solution.py:247
  11.5 0.0 copy-done
  11.5 0.0 copy-done.3
  11.5 0.0 copy-done.1
  11.5 0.0 copy-done.2
  11.5 2.7 %residuals.1 = f32[16,9,4,128]{3,2,1,0:T(4,128)S(1)} custom-call(bf16[2048,1024]{1,0:T(8,128)(2,1)S(1)} %get-tuple-element.7.x_ref, f32[3,2048,128]{2,1,0:T(8,128)S(1)} %get-tuple-element.8.ends_ref, bf16[64,2048]{1,0:T(8,128)(2,1)S(1)} %bitcast.3, f32[4,1,2048]{2,1,0:T(1,128)S(1)} %all_to_all.20.closes_ref, f32[1,2048]{1,0:T(1,128)S(1)} %bitcast.4, ...), custom_call_target="tpu_custom_call" | custom-call | tf_op jit(solution)/shard_map/residuals/pallas_call | solution.py:192
  14.2 15.8 %all_to_all.21 = f32[16,9,4,128]{3,2,1,0:T(4,128)S(1)} all-to-all(f32[16,9,4,128]{3,2,1,0:T(4,128)S(1)} %residuals.1), channel_id=1, replica_groups={{67,65,66,64,3,1,2,0,35,33,34,32,99,97,98,96},{71,69,70,68,7,5,6,4,39,3..., dimensions={0} | all-to-all | bytes 589824 | tf_op jit(solution)/shard_map/all_to_all | solution.py:247
  30.0 0.1 reduce_sum.18
  30.1 19.0 %all_to_all.22 = f32[8,9,4,128]{3,2,1,0:T(4,128)S(1)} all-to-all(f32[8,9,4,128]{3,2,1,0:T(4,128)S(1)} %broadcast_in_dim.4), channel_id=1, replica_groups={{22,0,8,4,30,26,12,18},{23,1,9,5,31,27,13,19},{20,2,10,6,28,24,14,16},{..., dimensions={0} | all-to-all | bytes 294912 | tf_op jit(solution)/shard_map/all_to_all | solution.py:247
  49.1 11.6 %all_to_all.23.in_ref = f32[16,9,4,128]{3,2,1,0:T(4,128)S(1)} all-to-all(f32[16,9,4,128]{3,2,1,0:T(4,128)S(1)} %broadcast_in_dim.5), channel_id=1, replica_groups={{67,65,66,64,3,1,2,0,35,33,34,32,99,97,98,96},{71,69,70,68,7,5,6,4,39,3..., dimensions={0} | all-to-all | bytes 589824 | tf_op jit(solution)/shard_map/all_to_all | solution.py:247
  60.7 1.0 %energies.1 = (f32[64,1024]{1,0:T(8,128)}, f32[1,1024]{1,0:T(1,128)}) custom-call(f32[16,9,4,128]{3,2,1,0:T(4,128)S(1)} %all_to_all.23.in_ref), custom_call_target="tpu_custom_call" | custom-call | tf_op jit(solution)/shard_map/energies/pallas_call | solution.py:204
  (3 shorter events, 0.1 us)
Async XLA Ops:
  0.6 10.9 %copy-start = (bf16[256,384]{1,0:T(8,128)(2,1)S(1)}, bf16[256,384]{1,0:T(8,128)(2,1)}, u32[]{:S(2)}) copy-start(bf16[256,384]{1,0:T(8,128)(2,1)} %constant.6.clone.weights_hbm.weights_ref) | copy-start | bytes 589828
  0.6 10.8 %copy-start.3 = (f32[1,256]{1,0:T(1,128)S(1)}, f32[1,256]{1,0:T(1,128)}, u32[]{:S(2)}) copy-start(f32[1,256]{1,0:T(1,128)} %constant.7.clone.step_ref) | copy-start | bytes 3076
  0.7 10.8 %copy-start.1 = (bf16[2048,64]{0,1:T(8,128)(2,1)S(1)}, bf16[2048,64]{0,1:T(8,128)(2,1)}, u32[]{:S(2)}) copy-start(bf16[2048,64]{0,1:T(8,128)(2,1)} %param.7) | copy-start | bytes 786436
  0.7 10.8 %copy-start.2 = (f32[2048]{0:T(1024)S(1)}, f32[2048]{0:T(1024)}, u32[]{:S(2)}) copy-start(f32[2048]{0:T(1024)} %param.6) | copy-start | bytes 24580

commit v8 on v7

--- a/solution.py
+++ b/solution.py
@@ -72,7 +72,7 @@
 
     line = start_ref[...] * weight([powers(width * p) for p in range(shards)])
     for s in range(shards - 1):
-        line += closes_ref[(s - TIME_FIRST) % shards] * weight(
+        line += closes_ref[TIME.index(s)] * weight(
             [powers(width * (p - 1 - s)) if s < p else 0.0 for p in range(shards)]
         )
     basis = ut_ref[...]
@@ -214,14 +214,9 @@
 
 ROWS = 512
 
-NEAR = (11, 9, 10, 8, 3, 1, 2, 0, 7, 5, 6, 4, 15, 13, 14, 12)
+NEAR = (11, 9, 8, 10, 3, 1, 0, 2, 7, 5, 4, 6, 15, 13, 12, 14)
 FAR = (5, 0, 2, 1, 7, 6, 3, 4)
-TIME_FIRST = 2
-
-
-def rotated(items, first):
-    items = list(items)
-    return items[first:] + items[:first]
+TIME = (2, 0, 3, 1)
 
 
 def stages(x_size, z_size, cores):
@@ -253,7 +248,7 @@
     pieces = len(near[0])
     weights, step = constants()
     close, ends, kept = call_closing(ROWS, shards, traffic, weights)
-    closes = exchange(close, "tm", [rotated(range(shards), TIME_FIRST)])
+    closes = exchange(close, "tm", [list(TIME)])
     part = call_residual(
         shards, pieces, kept, ends, subspace.T, closes, start_level.reshape(1, series), weights, step
     )

time: 61.9 us -> 61.7 us (level)
  no operation moved by 1% of the time
where the time goes in v8:
time: 61.7 us; the launch traced here: 61.4 us
  blocking collectives  53.7 us (87%)
  Pallas kernels  6.82 us (11%)
  between operations  0.7 us (1%)
    all_to_all x4, blocking collectives, exchange(): return lax.all_to_all(x, axis, 0, 0, axis_index_groups=groups, tiled=True)  53.7 us
    pallas_call x1, Pallas kernels, call_closing(): pl.pallas_call(functools.partial(closing_kernel, rows), in_specs=[HBM, HB...  3.18 us
    pallas_call x1, Pallas kernels, call_residual(): pl.pallas_call(functools.partial(residual_kernel, shards), in_specs=[VMEM...  2.69 us

profile of v8, /device:TPU:1, one launch (start us, length us, event | category | flops | bytes accessed | tf_op | source)
XLA Modules:
  0.0 61.4 jit_solution(12329411203676221754)
XLA Ops:
  0.6 0.0 copy-start
  0.6 0.0 copy-start.3
  0.7 0.0 copy-start.1
  0.7 0.0 copy-start.2
  0.7 3.2 %closing.1 = (f32[4,1,2048]{2,1,0:T(1,128)S(1)}, f32[3,2048,128]{2,1,0:T(8,128)S(1)}, bf16[2048,1024]{1,0:T(8,128)(2,1)S(1)}) custom-call(bf16[2048,1024]{1,0:T(8,128)(2,1)} %x_hbm.1, bf16[256,384]{1,0:T(8,128)(2,1)} %constant.6.clone.weights_hbm.weights_ref), custom_call_target="tpu_custom_call" | custom-call | tf_op jit(solution)/shard_map/closing/pallas_call | solution.py:169
  3.9 7.6 %all_to_all.20.closes_ref = f32[4,1,2048]{2,1,0:T(1,128)S(1)} all-to-all(f32[4,1,2048]{2,1,0:T(1,128)S(1)} %get-tuple-element.9), channel_id=1, replica_groups={{256,0,384,128},{257,1,385,129},{258,2,386,130},{259,3,387,131},{260,4,..., dimensions={0} | all-to-all | bytes 65536 | tf_op jit(solution)/shard_map/all_to_all | solution.py:242
  11.5 0.0 copy-done
  11.5 0.0 copy-done.3
  11.5 0.0 copy-done.1
  11.5 0.0 copy-done.2
  11.5 2.7 %residuals.1 = f32[16,9,4,128]{3,2,1,0:T(4,128)S(1)} custom-call(bf16[2048,1024]{1,0:T(8,128)(2,1)S(1)} %get-tuple-element.7.x_ref, f32[3,2048,128]{2,1,0:T(8,128)S(1)} %get-tuple-element.8.ends_ref, bf16[64,2048]{1,0:T(8,128)(2,1)S(1)} %bitcast.3, f32[4,1,2048]{2,1,0:T(1,128)S(1)} %all_to_all.20.closes_ref, f32[1,2048]{1,0:T(1,128)S(1)} %bitcast.4, ...), custom_call_target="tpu_custom_call" | custom-call | tf_op jit(solution)/shard_map/residuals/pallas_call | solution.py:192
  14.2 15.5 %all_to_all.21 = f32[16,9,4,128]{3,2,1,0:T(4,128)S(1)} all-to-all(f32[16,9,4,128]{3,2,1,0:T(4,128)S(1)} %residuals.1), channel_id=1, replica_groups={{67,65,64,66,3,1,0,2,35,33,32,34,99,97,96,98},{71,69,68,70,7,5,4,6,39,3..., dimensions={0} | all-to-all | bytes 589824 | tf_op jit(solution)/shard_map/all_to_all | solution.py:242
  29.7 0.1 reduce_sum.18
  29.8 18.1 %all_to_all.22 = f32[8,9,4,128]{3,2,1,0:T(4,128)S(1)} all-to-all(f32[8,9,4,128]{3,2,1,0:T(4,128)S(1)} %broadcast_in_dim.4), channel_id=1, replica_groups={{22,0,8,4,30,26,12,18},{23,1,9,5,31,27,13,19},{20,2,10,6,28,24,14,16},{..., dimensions={0} | all-to-all | bytes 294912 | tf_op jit(solution)/shard_map/all_to_all | solution.py:242
  47.9 12.5 %all_to_all.23.in_ref = f32[16,9,4,128]{3,2,1,0:T(4,128)S(1)} all-to-all(f32[16,9,4,128]{3,2,1,0:T(4,128)S(1)} %broadcast_in_dim.5), channel_id=1, replica_groups={{67,65,64,66,3,1,0,2,35,33,32,34,99,97,96,98},{71,69,68,70,7,5,4,6,39,3..., dimensions={0} | all-to-all | bytes 589824 | tf_op jit(solution)/shard_map/all_to_all | solution.py:242
  60.5 1.0 %energies.1 = (f32[64,1024]{1,0:T(8,128)}, f32[1,1024]{1,0:T(1,128)}) custom-call(f32[16,9,4,128]{3,2,1,0:T(4,128)S(1)} %all_to_all.23.in_ref), custom_call_target="tpu_custom_call" | custom-call | tf_op jit(solution)/shard_map/energies/pallas_call | solution.py:204
  (3 shorter events, 0.1 us)
Async XLA Ops:
  0.6 10.9 %copy-start = (bf16[256,384]{1,0:T(8,128)(2,1)S(1)}, bf16[256,384]{1,0:T(8,128)(2,1)}, u32[]{:S(2)}) copy-start(bf16[256,384]{1,0:T(8,128)(2,1)} %constant.6.clone.weights_hbm.weights_ref) | copy-start | bytes 589828
  0.6 10.8 %copy-start.3 = (f32[1,256]{1,0:T(1,128)S(1)}, f32[1,256]{1,0:T(1,128)}, u32[]{:S(2)}) copy-start(f32[1,256]{1,0:T(1,128)} %constant.7.clone.step_ref) | copy-start | bytes 3076
  0.7 10.8 %copy-start.1 = (bf16[2048,64]{0,1:T(8,128)(2,1)S(1)}, bf16[2048,64]{0,1:T(8,128)(2,1)}, u32[]{:S(2)}) copy-start(bf16[2048,64]{0,1:T(8,128)(2,1)} %param.7) | copy-start | bytes 786436
  0.7 10.8 %copy-start.2 = (f32[2048]{0:T(1024)S(1)}, f32[2048]{0:T(1024)}, u32[]{:S(2)}) copy-start(f32[2048]{0:T(1024)} %param.6) | copy-start | bytes 24580
